TPU v7x, 32 devices: a whole 2x2x4 slice. The times are simulated.
32 devices in a mesh: dp: 16 (over z, y, x), seq: 2 (over core).
Axes of the slice: x: 2, y: 2, z: 4, core: 2. Of those that a mesh axis runs over, the one named last changes fastest.
Arguments:
- tokens: bfloat16 [32, 1024, 768], P('dp', 'seq'), may hold values from -6 to 6
- segments: int32 [32, 1024], P('dp'), may hold values from 0 to 7, never falling along the last dimension, each value on 1 to 256 neighbouring positions
- query_weight: bfloat16 [768, 768], replicated, may hold values from -0.21875 to 0.21875
- query_bias: bfloat16 [768], replicated, may hold values from -1.75 to 1.75
- key_weight: bfloat16 [768, 768], replicated, may hold values from -0.21875 to 0.21875
- value_weight: bfloat16 [768, 768], replicated, may hold values from -0.21875 to 0.21875
- value_bias: bfloat16 [768], replicated, may hold values from -1.75 to 1.75
- output_weight: bfloat16 [768, 768], replicated, may hold values from -0.875 to 0.875
- output_bias: bfloat16 [768], replicated, may hold values from -1.75 to 1.75
- first_gain: bfloat16 [768], replicated, may hold values from 0.099609375 to 1.8984375
- first_shift: bfloat16 [768], replicated, may hold values from -1.75 to 1.75
- inner_weight: bfloat16 [768, 3072], replicated, may hold values from -0.21875 to 0.21875
- inner_bias: bfloat16 [3072], replicated, may hold values from -1.75 to 1.75
- outer_weight: bfloat16 [3072, 768], replicated, may hold values from -0.109375 to 0.109375
- outer_bias: bfloat16 [768], replicated, may hold values from -1.75 to 1.75
- second_gain: bfloat16 [768], replicated, may hold values from 0.099609375 to 1.8984375
- second_shift: bfloat16 [768], replicated, may hold values from -1.75 to 1.75
- cotangent: bfloat16 [32, 1024, 768], P('dp', 'seq'), may hold values from -6 to 6
Outputs:
- layer_out: bfloat16 [32, 1024, 768], P('dp', 'seq')
- tokens_grad: bfloat16 [32, 1024, 768], P('dp', 'seq')
- query_weight_grad: float32 [768, 768], P('dp')
- query_bias_grad: float32 [768], P('dp')
- key_weight_grad: float32 [768, 768], P('dp')
- value_weight_grad: float32 [768, 768], P('dp')
- value_bias_grad: float32 [768], P('dp')
- output_weight_grad: float32 [768, 768], P('dp')
- output_bias_grad: float32 [768], P('dp')
- first_gain_grad: float32 [768], P('dp')
- first_shift_grad: float32 [768], P('dp')
- inner_weight_grad: float32 [768, 3072], P('dp')
- inner_bias_grad: float32 [3072], P('dp')
- outer_weight_grad: float32 [3072, 768], P('dp')
- outer_bias_grad: float32 [768], P('dp')
- second_gain_grad: float32 [768], P('dp')
- second_shift_grad: float32 [768], P('dp')
Inputs may be any that keep to these rules, and one draw needn't show every extreme that they name: `segments`: along each row the ids never fall and every id appears; each id covers at most 256 positions; the positions with id 8 - 1 are padding.
All inputs are finite; a program needn't handle non-finite values.
Results may differ from a plain program's by a relative error of at most 0.015.
Values may be sent and summed in bfloat16 or wider, within the bound.
No kernel may reach another device: no remote copies, remote signals or barrier semaphores. Data moves between devices by JAX's collectives and lax.ppermute only.
A program may use at most 192 MiB of HBM per device.

v0:
```python
import jax
import jax.numpy as jnp
from jax import lax
from jax.sharding import PartitionSpec as P

HEAD_DIM = 64
DOCS = 8


def for_sending(array):

    def short(part):
        return part.astype(jnp.bfloat16) if part.dtype == jnp.float32 else part

    return jax.tree.map(short, array)


def layer_norm(summed, gain, shift):
    centre = summed - jnp.mean(summed, axis=-1, keepdims=True)
    spread = jnp.mean(centre * centre, axis=-1, keepdims=True)
    return centre * lax.rsqrt(spread + 1e-12) * gain + shift


def gelu_exact(inner):
    return jax.nn.gelu(inner, approximate=False)


def dense(left, right):
    return jnp.dot(left, right, preferred_element_type=jnp.float32)


def block_scores(query_block, heads_key, segment_block, segment_row):
    valid_keys = segment_row != DOCS - 1
    valid_block = segment_block != DOCS - 1
    allowed = (
        (segment_block[:, None] == segment_row[None, :])
        & valid_block[:, None]
        & valid_keys[None, :]
    )
    scores = (
        jnp.einsum("qhd,khd->hqk", query_block, heads_key, preferred_element_type=jnp.float32)
        * 0.125
    )
    return (scores, allowed[None], valid_block)


def attend_forward(item):
    query, key, value, segment_row = item
    length, local = query.shape
    heads = local // HEAD_DIM
    block = min(512, length)
    heads_query = query.reshape(length, heads, HEAD_DIM)
    heads_key = key.reshape(length, heads, HEAD_DIM)
    heads_value = value.reshape(length, heads, HEAD_DIM)
    pieces = []
    sums = []
    for start in range(0, length, block):
        scores, allowed, valid_block = block_scores(
            heads_query[start : start + block],
            heads_key,
            segment_row[start : start + block],
            segment_row,
        )
        largest = jnp.max(jnp.where(allowed, scores, -jnp.inf), axis=-1)
        safe_max = jnp.where(valid_block[None, :], largest, 0.0)
        weights = jnp.exp(jnp.where(allowed, scores - safe_max[..., None], -jnp.inf))
        total = jnp.sum(weights, axis=-1)
        safe_total = jnp.where(valid_block[None, :], total, 1.0)
        probs = (weights / safe_total[..., None]).astype(jnp.bfloat16)
        context = jnp.einsum("hqk,khd->qhd", probs, heads_value, preferred_element_type=jnp.float32)
        pieces.append(context.reshape(block, local).astype(jnp.bfloat16))
        sums.append(safe_max + jnp.log(safe_total))
    return (jnp.concatenate(pieces, axis=0), jnp.concatenate(sums, axis=1))


def attend_backward(item):
    query, key, value, segment_row, grad_context, logsum = item
    length, local = query.shape
    heads = local // HEAD_DIM
    block = min(512, length)
    heads_query = query.reshape(length, heads, HEAD_DIM)
    heads_key = key.reshape(length, heads, HEAD_DIM)
    heads_value = value.reshape(length, heads, HEAD_DIM)
    grad_key = jnp.zeros((length, heads, HEAD_DIM), jnp.float32)
    grad_value = jnp.zeros((length, heads, HEAD_DIM), jnp.float32)
    query_pieces = []
    for start in range(0, length, block):
        query_block = heads_query[start : start + block]
        scores, allowed, valid_block = block_scores(
            query_block, heads_key, segment_row[start : start + block], segment_row
        )
        probs = jnp.exp(
            jnp.where(allowed, scores - logsum[:, start : start + block][..., None], -jnp.inf)
        )
        probs_low = probs.astype(jnp.bfloat16)
        grad_block = grad_context[start : start + block].reshape(block, heads, HEAD_DIM)
        grad_probs = jnp.einsum(
            "qhd,khd->hqk", grad_block, heads_value, preferred_element_type=jnp.float32
        )
        grad_value = grad_value + jnp.einsum(
            "hqk,qhd->khd", probs_low, grad_block, preferred_element_type=jnp.float32
        )
        inner = jnp.sum(grad_probs * probs, axis=-1, keepdims=True)
        grad_scores = (probs * (grad_probs - inner)).astype(jnp.bfloat16)
        query_grad = (
            jnp.einsum("hqk,khd->qhd", grad_scores, heads_key, preferred_element_type=jnp.float32)
            * 0.125
        )
        query_pieces.append(query_grad.reshape(block, local).astype(jnp.bfloat16))
        grad_key = (
            grad_key
            + jnp.einsum(
                "hqk,qhd->khd", grad_scores, query_block, preferred_element_type=jnp.float32
            )
            * 0.125
        )
    return (
        jnp.concatenate(query_pieces, axis=0),
        grad_key.reshape(length, local).astype(jnp.bfloat16),
        grad_value.reshape(length, local).astype(jnp.bfloat16),
    )


def shards(
    tokens,
    segments,
    query_weight,
    query_bias,
    key_weight,
    value_weight,
    value_bias,
    output_weight,
    output_bias,
    first_gain,
    first_shift,
    inner_weight,
    inner_bias,
    outer_weight,
    outer_bias,
    second_gain,
    second_shift,
    cotangent,
):
    rows, half, width = tokens.shape
    flattened = tokens.reshape(rows * half, width)
    query = (
        (dense(flattened, query_weight) + query_bias.astype(jnp.float32))
        .astype(jnp.bfloat16)
        .reshape(rows, half, width)
    )
    key = dense(flattened, key_weight).astype(jnp.bfloat16).reshape(rows, half, width)
    value = (
        (dense(flattened, value_weight) + value_bias.astype(jnp.float32))
        .astype(jnp.bfloat16)
        .reshape(rows, half, width)
    )
    heads_query, heads_key, heads_value = (
        lax.all_to_all(query, "seq", split_axis=2, concat_axis=1, tiled=True),
        lax.all_to_all(key, "seq", split_axis=2, concat_axis=1, tiled=True),
        lax.all_to_all(value, "seq", split_axis=2, concat_axis=1, tiled=True),
    )
    context, logsum = lax.map(attend_forward, (heads_query, heads_key, heads_value, segments))
    context_tokens = jax.tree.map(
        lambda part, own: part.astype(own.dtype),
        lax.all_to_all(for_sending(context), "seq", split_axis=1, concat_axis=2, tiled=True),
        context,
    )
    context_rows = context_tokens.reshape(rows * half, width)
    attended = dense(context_rows, output_weight) + output_bias.astype(jnp.float32)
    first_sum = flattened.astype(jnp.float32) + attended
    first_norm, first_back = jax.vjp(
        layer_norm, first_sum, first_gain.astype(jnp.float32), first_shift.astype(jnp.float32)
    )
    norm_low = first_norm.astype(jnp.bfloat16)
    inner = dense(norm_low, inner_weight) + inner_bias.astype(jnp.float32)
    activation, gelu_back = jax.vjp(gelu_exact, inner)
    act_low = activation.astype(jnp.bfloat16)
    outer = dense(act_low, outer_weight) + outer_bias.astype(jnp.float32)
    second_sum = first_norm + outer
    result, second_back = jax.vjp(
        layer_norm, second_sum, second_gain.astype(jnp.float32), second_shift.astype(jnp.float32)
    )
    layer_out = result.astype(jnp.bfloat16).reshape(rows, half, width)
    grad_result = cotangent.reshape(rows * half, width).astype(jnp.float32)
    grad_second, second_gain_term, second_shift_term = second_back(grad_result)
    grad_outer = grad_second.astype(jnp.bfloat16)
    outer_weight_term = dense(act_low.T, grad_outer)
    outer_bias_term = jnp.sum(grad_outer.astype(jnp.float32), axis=0)
    (grad_inner_full,) = gelu_back(dense(grad_outer, outer_weight.T))
    grad_inner = grad_inner_full.astype(jnp.bfloat16)
    inner_weight_term = dense(norm_low.T, grad_inner)
    inner_bias_term = jnp.sum(grad_inner.astype(jnp.float32), axis=0)
    grad_norm = grad_second + dense(grad_inner, inner_weight.T)
    grad_first, first_gain_term, first_shift_term = first_back(grad_norm)
    grad_attn = grad_first.astype(jnp.bfloat16)
    output_weight_term = dense(context_rows.T, grad_attn)
    output_bias_term = jnp.sum(grad_attn.astype(jnp.float32), axis=0)
    grad_context = dense(grad_attn, output_weight.T).astype(jnp.bfloat16).reshape(rows, half, width)
    heads_grad = lax.all_to_all(grad_context, "seq", split_axis=2, concat_axis=1, tiled=True)
    grad_query, grad_key, grad_value = lax.map(
        attend_backward, (heads_query, heads_key, heads_value, segments, heads_grad, logsum)
    )
    token_query, token_key, token_value = (
        lax.all_to_all(
            for_sending(grad_query), "seq", split_axis=1, concat_axis=2, tiled=True
        ).astype(grad_query.dtype),
        lax.all_to_all(
            for_sending(grad_key), "seq", split_axis=1, concat_axis=2, tiled=True
        ).astype(grad_key.dtype),
        lax.all_to_all(
            for_sending(grad_value), "seq", split_axis=1, concat_axis=2, tiled=True
        ).astype(grad_value.dtype),
    )
    token_query = token_query.reshape(rows * half, width)
    token_key = token_key.reshape(rows * half, width)
    token_value = token_value.reshape(rows * half, width)
    query_weight_term = dense(flattened.T, token_query)
    query_bias_term = jnp.sum(token_query.astype(jnp.float32), axis=0)
    key_weight_term = dense(flattened.T, token_key)
    value_weight_term = dense(flattened.T, token_value)
    value_bias_term = jnp.sum(token_value.astype(jnp.float32), axis=0)
    tokens_grad = (
        grad_first
        + dense(token_query, query_weight.T)
        + dense(token_key, key_weight.T)
        + dense(token_value, value_weight.T)
    )
    tokens_grad = tokens_grad.astype(jnp.bfloat16).reshape(rows, half, width)
    parted = (
        lax.psum_scatter(query_weight_term, "dp", scatter_dimension=0, tiled=True),
        lax.psum_scatter(query_bias_term, "dp", scatter_dimension=0, tiled=True),
        lax.psum_scatter(key_weight_term, "dp", scatter_dimension=0, tiled=True),
        lax.psum_scatter(value_weight_term, "dp", scatter_dimension=0, tiled=True),
        lax.psum_scatter(value_bias_term, "dp", scatter_dimension=0, tiled=True),
        lax.psum_scatter(output_weight_term, "dp", scatter_dimension=0, tiled=True),
        lax.psum_scatter(output_bias_term, "dp", scatter_dimension=0, tiled=True),
        lax.psum_scatter(first_gain_term, "dp", scatter_dimension=0, tiled=True),
        lax.psum_scatter(first_shift_term, "dp", scatter_dimension=0, tiled=True),
        lax.psum_scatter(inner_weight_term, "dp", scatter_dimension=0, tiled=True),
        lax.psum_scatter(inner_bias_term, "dp", scatter_dimension=0, tiled=True),
        lax.psum_scatter(outer_weight_term, "dp", scatter_dimension=0, tiled=True),
        lax.psum_scatter(outer_bias_term, "dp", scatter_dimension=0, tiled=True),
        lax.psum_scatter(second_gain_term, "dp", scatter_dimension=0, tiled=True),
        lax.psum_scatter(second_shift_term, "dp", scatter_dimension=0, tiled=True),
    )
    summed = (
        lax.psum(parted[0].astype(jnp.bfloat16), "seq").astype(jnp.float32),
        lax.psum(parted[1].astype(jnp.bfloat16), "seq").astype(jnp.float32),
        lax.psum(parted[2].astype(jnp.bfloat16), "seq").astype(jnp.float32),
        lax.psum(parted[3].astype(jnp.bfloat16), "seq").astype(jnp.float32),
        lax.psum(parted[4].astype(jnp.bfloat16), "seq").astype(jnp.float32),
        lax.psum(parted[5].astype(jnp.bfloat16), "seq").astype(jnp.float32),
        lax.psum(parted[6].astype(jnp.bfloat16), "seq").astype(jnp.float32),
        lax.psum(parted[7].astype(jnp.bfloat16), "seq").astype(jnp.float32),
        lax.psum(parted[8].astype(jnp.bfloat16), "seq").astype(jnp.float32),
        lax.psum(parted[9].astype(jnp.bfloat16), "seq").astype(jnp.float32),
        lax.psum(parted[10].astype(jnp.bfloat16), "seq").astype(jnp.float32),
        lax.psum(parted[11].astype(jnp.bfloat16), "seq").astype(jnp.float32),
        lax.psum(parted[12].astype(jnp.bfloat16), "seq").astype(jnp.float32),
        lax.psum(parted[13].astype(jnp.bfloat16), "seq").astype(jnp.float32),
        lax.psum(parted[14].astype(jnp.bfloat16), "seq").astype(jnp.float32),
    )
    return (
        layer_out,
        tokens_grad,
        summed[0],
        summed[1],
        summed[2],
        summed[3],
        summed[4],
        summed[5],
        summed[6],
        summed[7],
        summed[8],
        summed[9],
        summed[10],
        summed[11],
        summed[12],
        summed[13],
        summed[14],
    )


def solution(mesh):
    return jax.shard_map(
        shards,
        mesh=mesh,
        in_specs=(
            P("dp", "seq", None),
            P("dp", None),
            P(),
            P(),
            P(),
            P(),
            P(),
            P(),
            P(),
            P(),
            P(),
            P(),
            P(),
            P(),
            P(),
            P(),
            P(),
            P("dp", "seq", None),
        ),
        out_specs=(
            P("dp", "seq", None),
            P("dp", "seq", None),
            P("dp", None),
            P("dp"),
            P("dp", None),
            P("dp", None),
            P("dp"),
            P("dp", None),
            P("dp"),
            P("dp"),
            P("dp"),
            P("dp", None),
            P("dp"),
            P("dp", None),
            P("dp"),
            P("dp"),
            P("dp"),
        ),
        check_vma=False,
    )
```

profile of v0, /device:TPU:0, one launch (start us, length us, event | category | flops | bytes accessed | tf_op | source)
XLA Modules:
  0.0 1264.8 jit_solution(12221569576437564846)
XLA Ops:
  22.2 4.9 copy.53
  27.1 4.6 all-to-all-start
  41.6 4.9 copy.57
  46.5 4.6 all-to-all-start.2
  68.5 50.8 %while.26 = (s32[]{:T(128)}, bf16[2,1024,384]{1,2,0:T(8,128)(2,1)}, f32[2,6,1024]{2,1,0:T(8,128)S(1)}, bf16[2,1024,384]{1,2,0:T(8,128)(2,1)}, s32[2,1024]{1,0:T(...) while((s32[]{:T(128)}, bf16[2,1024,384]{1,2,0:T(8,128)(2,1)}, ...), condition=%wide.region_5.6_spmd, body=%wide.region_0.5_spmd.sunk | while | flops 1691243520 | bytes 91074184 | solution.py:162
  84.2 4.4 fusion.166
  88.6 4.4 fusion.164
  109.5 4.4 fusion.166
  113.9 4.4 fusion.164
  119.3 5.1 copy.59
  124.4 6.6 all_to_all.132
  137.4 35.2 %multiply_convert_fusion.3 = (bf16[1024,3072]{1,0:T(8,128)(2,1)S(1)}, f32[1024,3072]{1,0:T(8,128)}, f32[1024,3072]{1,0:T(8,128)}) fusion(f32[3072]{0:T(1024)S(1)} %convert_element_type.275, bf16[768,3072]{1,0:T(8,128)(2,1)S(1)} %bitcast.344, f32[1024,768]{1,0:T(8,128)S(1)} %get-tuple-element.282, f32[768]{0:T(1024)S(1)} %convert_element_type.273, ...), kind=kOutput, calls=%fused_computation.83 | convolution fusion | flops 5043388416 | bytes 39348224 | tf_op jit(solution)/shard_map/dot_general | solution.py:29
  172.6 5.5 fusion.51
  186.5 17.9 %convert_reduce_fusion = (f32[3072]{0:T(1024)}, bf16[1024,3072]{1,0:T(8,128)(2,1)}) fusion(f32[1024,3072]{1,0:T(8,128)} %get-tuple-element.249, bf16[1024,768]{1,0:T(8,128)(2,1)S(1)} %get-tuple-element.241, bf16[3072,768]{1,0:T(8,128)(2,1)} %param.35, f32[1024,3072]{1,0:T(8,128)} %get-tuple-element.283, f32[3072]{0:T(1024)S(1)} %convert_element_type.275), kind=kOutput, calls=%fused_computation.81 | convolution fusion | flops 4885312512 | bytes 37773312 | tf_op jit(solution)/shard_map/dot_general | solution.py:29
  204.3 11.0 multiply_reduce_fusion.2
  245.2 138.6 %while.27 = (s32[]{:T(128)}, bf16[2,1024,384]{1,2,0:T(8,128)(2,1)}, bf16[2,1024,384]{1,2,0:T(8,128)(2,1)}, bf16[2,1024,384]{1,2,0:T(8,128)(2,1)}, bf16[2,1024,38...) while((s32[]{:T(128)}, bf16[2,1024,384]{1,2,0:T(8,128)(2,1)}, ...), condition=%wide.region_17.18_spmd, body=%wide.region_14.17_spmd.sunk | while | flops 4128370688 | bytes 326100096 | solution.py:200
  252.6 7.1 multiply_reduce_fusion.9
  259.7 7.0 multiply_convert_fusion.8
  271.7 8.2 multiply_reduce_fusion.8
  279.9 9.9 multiply_convert_fusion.7
  289.7 4.5 multiply_convert_fusion.9
  295.2 5.0 fusion.193
  302.3 4.5 fusion.194
  306.8 5.1 add_convert_fusion.11
  321.6 7.1 multiply_reduce_fusion.9
  328.8 7.0 multiply_convert_fusion.8
  340.8 8.2 multiply_reduce_fusion.8
  348.9 9.9 multiply_convert_fusion.7
  358.8 4.4 multiply_convert_fusion.9
  364.2 5.0 fusion.193
  371.3 4.5 fusion.194
  375.7 5.1 add_convert_fusion.11
  383.8 5.0 copy.63
  388.8 6.1 all_to_all.133
  404.1 4.9 copy.65
  409.0 6.1 all_to_all.134
  424.2 5.0 copy.67
  429.2 6.3 all_to_all.135
  444.7 11.0 fusion.42
  455.8 10.0 fusion.58
  472.8 5.0 fusion.55
  482.7 53.6 %reduce-scatter.19.cloned.1.call-done = f32[48,768]{1,0:T(8,128)} async-done(((f32[768,768]{1,0:T(8,128)}), f32[48,768]{1,0:T(8,128)}) %reduce-scatter.19.cloned.1.call-update) | async-done | bytes 147472
  538.0 131.6 %reduce-scatter.21.cloned.1.call-done = f32[48,768]{1,0:T(8,128)} async-done(((f32[768,768]{1,0:T(8,128)}), f32[48,768]{1,0:T(8,128)}) %reduce-scatter.21.cloned.1.call-update) | async-done | bytes 147472
  671.3 131.5 %reduce-scatter.23.cloned.1.call-done = f32[48,768]{1,0:T(8,128)} async-done(((f32[768,768]{1,0:T(8,128)}), f32[48,768]{1,0:T(8,128)}) %reduce-scatter.23.cloned.1.call-update) | async-done | bytes 147472
  804.6 174.2 %reduce-scatter.15.cloned.1.call-done = f32[48,3072]{1,0:T(8,128)} async-done(((f32[768,3072]{1,0:T(8,128)}), f32[48,3072]{1,0:T(8,128)}) %reduce-scatter.15.cloned.1.call-update) | async-done | bytes 589840 | tf_op jit(solution)/shard_map/reduce_scatter | solution.py:239
  980.6 174.4 %reduce-scatter.17.cloned.1.call-done = f32[192,768]{1,0:T(8,128)} async-done(((f32[3072,768]{1,0:T(8,128)}), f32[192,768]{1,0:T(8,128)}) %reduce-scatter.17.cloned.1.call-update) | async-done | bytes 589840 | tf_op jit(solution)/shard_map/reduce_scatter | solution.py:241
  1157.1 75.3 %all-reduce.9 = (bf16[768]{0:T(1024)(128)(2,1)S(1)}, bf16[768]{0:T(1024)(128)(2,1)S(1)}, bf16[768]{0:T(1024)(128)(2,1)S(1)}, bf16[768]{0:T(1024)(128)(2,1)S(1)},...) all-reduce(f32[768]{0:T(1024)S(1)} %reduce_sum.234, ...), channel_id=3, replica_groups=mesh['dp'=16,'seq'=2] {'dp'}, use_global_device_ids=true, to_apply=%region_21.22.clone | all-reduce | flops 9216 | bytes 55296
  1240.2 7.3 add_convert_fusion.2
  (359 shorter events, 219.7 us)
Async XLA Ops:
  7.2 125.8 %copy-start = (bf16[768,768]{1,0:T(8,128)(2,1)S(1)}, bf16[768,768]{1,0:T(8,128)(2,1)}, u32[]{:S(2)}) copy-start(bf16[768,768]{1,0:T(8,128)(2,1)} %param.29) | copy-start | bytes 3538948
  11.1 6.7 copy-start.53
  14.2 12.9 %all-to-all-start.1 = ((bf16[2,512,768]{1,0,2:T(2,128)(2,1)}), bf16[2,512,768]{1,0,2:T(2,128)(2,1)S(1)}, u32[]{:S(2)}, u32[]{:S(2)}) async-start(bf16[2,512,768]{1,0,2:T(2,128)(2,1)} %copy.55), calls=%async_computation.1 | async-start | bytes 3145728 | tf_op jit(solution)/shard_map/all_to_all | solution.py:158
  27.1 19.4 %all-to-all-start = ((bf16[2,512,768]{1,0,2:T(2,128)(2,1)}), bf16[2,512,768]{1,0,2:T(2,128)(2,1)}, u32[]{:S(2)}, u32[]{:S(2)}) async-start(bf16[2,512,768]{1,0,2:T(2,128)(2,1)} %copy.53), calls=%async_computation | async-start | bytes 3145728 | tf_op jit(solution)/shard_map/all_to_all | solution.py:160
  46.5 12.7 %all-to-all-start.2 = ((bf16[2,512,768]{1,0,2:T(2,128)(2,1)}), bf16[2,512,768]{1,0,2:T(2,128)(2,1)}, u32[]{:S(2)}, u32[]{:S(2)}) async-start(bf16[2,512,768]{1,0,2:T(2,128)(2,1)} %copy.57), calls=%async_computation.2 | async-start | bytes 3145728 | tf_op jit(solution)/shard_map/all_to_all | solution.py:159
  51.1 429.9 %reduce-scatter.13.cloned.1.call-start = ((), (), s32[]{:S(2)}) async-start(), calls=%async_computation.14 | async-start | bytes 2506752 | tf_op jit(solution)/shard_map/reduce_scatter | solution.py:235
  63.4 5.2 copy-start.32
  119.3 11.7 copy-start.7
  119.3 11.7 copy-start.34
  133.0 39.6 %slice-start = ((s8[4718592]{0:T(1024)(128)(4,1)}), s8[4194304]{0:T(1024)(128)(4,1)S(1)}, s32[]{:S(2)}) async-start(s8[4718592]{0:T(1024)(128)(4,1)} %bitcast.341), calls=%async_computation.21 | async-start | bytes 8388608
  134.6 80.7 %copy-start.12 = (f32[1024,768]{1,0:T(8,128)}, f32[1024,768]{1,0:T(8,128)S(1)}, u32[]{:S(2)}) copy-start(f32[1024,768]{1,0:T(8,128)S(1)} %get-tuple-element.282) | copy-start | bytes 9437188
  134.7 80.7 %copy-start.36 = (f32[1024]{0:T(1024)}, f32[1024]{0:T(1024)S(1)}, u32[]{:S(2)}) copy-start(f32[1024]{0:T(1024)S(1)} %broadcast_multiply_fusion.1) | copy-start | bytes 12292
  137.2 78.1 %copy-start.38 = (f32[1024]{0:T(1024)}, f32[1024]{0:T(1024)S(1)}, u32[]{:S(2)}) copy-start(f32[1024]{0:T(1024)S(1)} %fusion.40) | copy-start | bytes 12292
  137.3 78.1 %copy-start.40 = (f32[768]{0:T(1024)}, f32[768]{0:T(1024)S(1)}, u32[]{:S(2)}) copy-start(f32[768]{0:T(1024)S(1)} %convert_element_type.272) | copy-start | bytes 9220
  137.3 35.3 %copy-start.42 = (f32[768]{0:T(1024)}, f32[768]{0:T(1024)S(1)}, u32[]{:S(2)}) copy-start(f32[768]{0:T(1024)S(1)} %convert_element_type.273) | copy-start | bytes 9220
  137.4 35.2 %slice-start.1 = ((s8[4718592]{0:T(1024)(128)(4,1)}), s8[524288]{0:T(1024)(128)(4,1)S(1)}, s32[]{:S(2)}) async-start(s8[4718592]{0:T(1024)(128)(4,1)} %bitcast.341), calls=%async_computation.22 | async-start | bytes 1048576
  172.6 5.5 copy-start.66
  186.5 17.9 %copy-start.30 = (bf16[1024,768]{1,0:T(8,128)(2,1)}, bf16[1024,768]{1,0:T(8,128)(2,1)S(1)}, u32[]{:S(2)}) copy-start(bf16[1024,768]{1,0:T(8,128)(2,1)S(1)} %get-tuple-element.241) | copy-start | bytes 4718596
  229.4 6.2 all-to-all-start.4
  233.0 303.2 %reduce-scatter.19.cloned.1.call-start = ((), (), s32[]{:S(2)}) async-start(), calls=%async_computation.17 | async-start | bytes 2506752
  245.4 6.3 copy-start.14
  247.2 12.5 copy-start.4
  252.5 7.2 copy-start.9
  295.2 5.0 copy-start.3
  306.8 5.1 copy-start.21
  306.8 5.1 copy-start.23
  314.4 6.2 copy-start.14
  316.3 12.5 copy-start.4
  321.5 7.2 copy-start.9
  375.7 5.1 copy-start.21
  375.7 5.1 copy-start.23
  404.0 265.6 %reduce-scatter.21.cloned.1.call-start = ((), (), s32[]{:S(2)}) async-start(), calls=%async_computation.18 | async-start | bytes 2506752
  424.2 378.7 %reduce-scatter.23.cloned.1.call-start = ((), (), s32[]{:S(2)}) async-start(), calls=%async_computation.19 | async-start | bytes 2506752
  444.6 534.1 %reduce-scatter.15.cloned.1.call-start = ((), (), s32[]{:S(2)}) async-start(), calls=%async_computation.15 | async-start | bytes 10027008 | tf_op jit(solution)/shard_map/reduce_scatter | solution.py:239
  455.8 699.2 %reduce-scatter.17.cloned.1.call-start = ((), (), s32[]{:S(2)}) async-start(), calls=%async_computation.16 | async-start | bytes 10027008 | tf_op jit(solution)/shard_map/reduce_scatter | solution.py:241
  465.8 5.0 copy-start.65
  465.8 781.6 %all-reduce.14.cloned.1.call-start = ((), (), s32[]{:S(2)}) async-start(), calls=%async_computation.20 | async-start | bytes 2506752 | tf_op jit(solution)/shard_map/psum | solution.py:247
  472.8 5.0 copy-start.27
  472.8 5.0 copy-start.64
  480.9 675.9 %copy-start.18 = (bf16[2,512,768]{2,1,0:T(8,128)(2,1)S(1)}, bf16[2,512,768]{2,1,0:T(8,128)(2,1)}, u32[]{:S(2)}) copy-start(bf16[2,512,768]{2,1,0:T(8,128)(2,1)} %param.39) | copy-start | bytes 4718596
  480.9 676.1 %copy-start.46 = (f32[768]{0:T(1024)S(1)}, f32[768]{0:T(1024)}, u32[]{:S(2)}) copy-start(f32[768]{0:T(1024)} %get-tuple-element.240) | copy-start | bytes 9220
  480.9 676.2 %copy-start.47 = (f32[768]{0:T(1024)S(1)}, f32[768]{0:T(1024)}, u32[]{:S(2)}) copy-start(f32[768]{0:T(1024)} %get-tuple-element.242) | copy-start | bytes 9220
  480.9 676.2 %copy-start.48 = (f32[768]{0:T(1024)S(1)}, f32[768]{0:T(1024)}, u32[]{:S(2)}) copy-start(f32[768]{0:T(1024)} %get-tuple-element.167) | copy-start | bytes 9220
  480.9 676.2 %copy-start.49 = (f32[3072]{0:T(1024)S(1)}, f32[3072]{0:T(1024)}, u32[]{:S(2)}) copy-start(f32[3072]{0:T(1024)} %get-tuple-element.287) | copy-start | bytes 36868
  481.0 676.2 %copy-start.51 = (f32[768]{0:T(1024)S(1)}, f32[768]{0:T(1024)}, u32[]{:S(2)}) copy-start(f32[768]{0:T(1024)} %get-tuple-element.165) | copy-start | bytes 9220
  481.0 676.2 %copy-start.52 = (f32[768]{0:T(1024)S(1)}, f32[768]{0:T(1024)}, u32[]{:S(2)}) copy-start(f32[768]{0:T(1024)} %get-tuple-element.169) | copy-start | bytes 9220
  481.0 759.2 %copy-start.45 = (f32[1024]{0:T(1024)S(1)}, f32[1024]{0:T(1024)}, u32[]{:S(2)}) copy-start(f32[1024]{0:T(1024)} %copy-done.44) | copy-start | bytes 12292
  1240.2 17.6 %copy-start.1 = (bf16[768,768]{1,0:T(8,128)(2,1)S(1)}, bf16[768,768]{1,0:T(8,128)(2,1)}, u32[]{:S(2)}) copy-start(bf16[768,768]{1,0:T(8,128)(2,1)} %param.29) | copy-start | bytes 3538948
  (49 other events, 128.6 us)
Sparse Core Ops, SparseCore 0:
  223.6 132.1 reduce-scatter.12
  404.1 132.1 reduce-scatter.18
  541.2 128.3 reduce-scatter.20
  674.4 128.4 reduce-scatter.22
  808.4 170.3 reduce-scatter.14
  984.3 170.6 reduce-scatter.16
  1158.9 19.4 all-reduce.13
where the time goes:
time: 1270 us; the launch traced here: 1260 us
  waiting for transfers between devices  668 us (53%)
  matrix products  246 us (19%)
  local copies, waits for them, and re-layouts  125 us (10%)
  blocking collectives  103 us (8%)
  other arithmetic  87.9 us (7%)
  starting transfers between devices  17.1 us (1%)
  between operations  16.5 us (1%)
    unnamed x10, waiting for transfers between devices  317 us
    reduce_scatter x1, waiting for transfers between devices, shards(): lax.psum_scatter(outer_weight_term, 'dp', scatter_dimension=0, tiled=True)  174 us
    reduce_scatter x1, waiting for transfers between devices, shards(): lax.psum_scatter(inner_weight_term, 'dp', scatter_dimension=0, tiled=True)  174 us
    dot_general x18, matrix products, dense(): return jnp.dot(left, right, preferred_element_type=jnp.float32)  133 us
    unnamed x1, blocking collectives  75.3 us
    convert_element_type x4, other arithmetic, attend_backward(): grad_scores = (probs * (grad_probs - inner)).astype(jnp.bfloat16)  33.7 us
    unnamed x135, local copies, waits for them, and re-layouts  33 us
    dot_general x4, matrix products, attend_backward(): jnp.einsum('qhd,khd->hqk', grad_block, heads_value, preferred_element_typ...  30.6 us
  transfers between devices with their start and end apart: 11, of which 6 were waited for; matrix products, arithmetic and copies ran while one was open for 21% of the time, Pallas kernels for 0%

commit v1 on v0

v1 whole, which is shorter than its diff:
```python
import jax
import jax.numpy as jnp
from jax import lax
from jax.sharding import PartitionSpec as P

HEAD_DIM = 64
DOCS = 8
SWAP = [(0, 1), (1, 0)]


def layer_norm(summed, gain, shift):
    centre = summed - jnp.mean(summed, axis=-1, keepdims=True)
    spread = jnp.mean(centre * centre, axis=-1, keepdims=True)
    return centre * lax.rsqrt(spread + 1e-12) * gain + shift


def gelu_exact(inner):
    return jax.nn.gelu(inner, approximate=False)


def dense(left, right):
    return jnp.dot(left, right, preferred_element_type=jnp.float32)


def block_scores(query_block, heads_key, segment_block, segment_row):
    valid_keys = segment_row != DOCS - 1
    valid_block = segment_block != DOCS - 1
    allowed = (
        (segment_block[:, None] == segment_row[None, :])
        & valid_block[:, None]
        & valid_keys[None, :]
    )
    scores = (
        jnp.einsum("qhd,khd->hqk", query_block, heads_key, preferred_element_type=jnp.float32)
        * 0.125
    )
    return (scores, allowed[None], valid_block)


def attend_forward(item):
    query, key, value, segment_row = item
    length, local = query.shape
    heads = local // HEAD_DIM
    block = min(512, length)
    heads_query = query.reshape(length, heads, HEAD_DIM)
    heads_key = key.reshape(length, heads, HEAD_DIM)
    heads_value = value.reshape(length, heads, HEAD_DIM)
    pieces = []
    sums = []
    for start in range(0, length, block):
        scores, allowed, valid_block = block_scores(
            heads_query[start : start + block],
            heads_key,
            segment_row[start : start + block],
            segment_row,
        )
        largest = jnp.max(jnp.where(allowed, scores, -jnp.inf), axis=-1)
        safe_max = jnp.where(valid_block[None, :], largest, 0.0)
        weights = jnp.exp(jnp.where(allowed, scores - safe_max[..., None], -jnp.inf))
        total = jnp.sum(weights, axis=-1)
        safe_total = jnp.where(valid_block[None, :], total, 1.0)
        probs = (weights / safe_total[..., None]).astype(jnp.bfloat16)
        context = jnp.einsum("hqk,khd->qhd", probs, heads_value, preferred_element_type=jnp.float32)
        pieces.append(context.reshape(block, local).astype(jnp.bfloat16))
        sums.append(safe_max + jnp.log(safe_total))
    return (jnp.concatenate(pieces, axis=0), jnp.concatenate(sums, axis=1))


def attend_backward(item):
    query, key, value, segment_row, grad_context, logsum = item
    length, local = query.shape
    heads = local // HEAD_DIM
    block = min(512, length)
    heads_query = query.reshape(length, heads, HEAD_DIM)
    heads_key = key.reshape(length, heads, HEAD_DIM)
    heads_value = value.reshape(length, heads, HEAD_DIM)
    grad_key = jnp.zeros((length, heads, HEAD_DIM), jnp.float32)
    grad_value = jnp.zeros((length, heads, HEAD_DIM), jnp.float32)
    query_pieces = []
    for start in range(0, length, block):
        query_block = heads_query[start : start + block]
        scores, allowed, valid_block = block_scores(
            query_block, heads_key, segment_row[start : start + block], segment_row
        )
        probs = jnp.exp(
            jnp.where(allowed, scores - logsum[:, start : start + block][..., None], -jnp.inf)
        )
        probs_low = probs.astype(jnp.bfloat16)
        grad_block = grad_context[start : start + block].reshape(block, heads, HEAD_DIM)
        grad_probs = jnp.einsum(
            "qhd,khd->hqk", grad_block, heads_value, preferred_element_type=jnp.float32
        )
        grad_value = grad_value + jnp.einsum(
            "hqk,qhd->khd", probs_low, grad_block, preferred_element_type=jnp.float32
        )
        inner = jnp.sum(grad_probs * probs, axis=-1, keepdims=True)
        grad_scores = (probs * (grad_probs - inner)).astype(jnp.bfloat16)
        query_grad = (
            jnp.einsum("hqk,khd->qhd", grad_scores, heads_key, preferred_element_type=jnp.float32)
            * 0.125
        )
        query_pieces.append(query_grad.reshape(block, local).astype(jnp.bfloat16))
        grad_key = (
            grad_key
            + jnp.einsum(
                "hqk,qhd->khd", grad_scores, query_block, preferred_element_type=jnp.float32
            )
            * 0.125
        )
    return (
        jnp.concatenate(query_pieces, axis=0),
        grad_key.reshape(length, local).astype(jnp.bfloat16),
        grad_value.reshape(length, local).astype(jnp.bfloat16),
    )


def pick(array, index, axis):
    return lax.dynamic_index_in_dim(array, index, axis, keepdims=False)


def total_of(parts):
    result = parts[0].astype(jnp.float32)
    for part in parts[1:]:
        result = result + part.astype(jnp.float32)
    return result


def scatter_sum(term, order):
    size = lax.axis_size("dp")
    me = lax.axis_index("dp")
    core = lax.axis_index("seq")
    bits = size.bit_length() - 1
    rows, columns = term.shape
    own = rows // size // 2
    term = term.reshape((2,) * bits + (2, own, columns))
    sent = pick(term, 1 - core, bits).astype(jnp.bfloat16)
    parts = [pick(term, core, bits), lax.ppermute(sent, "seq", SWAP)]
    left = list(range(bits - 1, -1, -1))
    for bit in [b for b in order if b < bits] + [b for b in range(bits) if b not in order]:
        axis = left.index(bit)
        mine = (me >> bit) & 1
        sent = total_of([pick(part, 1 - mine, axis) for part in parts]).astype(jnp.bfloat16)
        got = lax.ppermute(sent, "dp", [(i, i ^ (1 << bit)) for i in range(size)])
        parts = [pick(part, mine, axis) for part in parts] + [got]
        left.remove(bit)
    half = total_of(parts)
    other = lax.ppermute(half, "seq", SWAP)
    first = jnp.where(core == 0, half, other)
    second = jnp.where(core == 0, other, half)
    return jnp.concatenate([first, second], axis=0)


def shards(
    tokens,
    segments,
    query_weight,
    query_bias,
    key_weight,
    value_weight,
    value_bias,
    output_weight,
    output_bias,
    first_gain,
    first_shift,
    inner_weight,
    inner_bias,
    outer_weight,
    outer_bias,
    second_gain,
    second_shift,
    cotangent,
):
    rows, half, width = tokens.shape
    core = lax.axis_index("seq")
    size = lax.axis_size("dp")

    def whole_row(array):
        mine = pick(array, core, 0)
        other = lax.ppermute(pick(array, 1 - core, 0), "seq", SWAP)
        first = jnp.where(core == 0, mine, other)
        second = jnp.where(core == 0, other, mine)
        return jnp.concatenate([first, second], axis=0)

    def own_halves(array):
        array = array.reshape(2, half, width)
        mine = pick(array, core, 0)
        other = lax.ppermute(pick(array, 1 - core, 0), "seq", SWAP)
        first = jnp.where(core == 0, mine, other)
        second = jnp.where(core == 0, other, mine)
        return jnp.stack([first, second], axis=0)

    flattened = whole_row(tokens)
    grad_result = whole_row(cotangent).astype(jnp.float32)
    segment_row = pick(segments, core, 0)
    query = (dense(flattened, query_weight) + query_bias.astype(jnp.float32)).astype(jnp.bfloat16)
    key = dense(flattened, key_weight).astype(jnp.bfloat16)
    value = (dense(flattened, value_weight) + value_bias.astype(jnp.float32)).astype(jnp.bfloat16)
    context_rows, logsum = attend_forward((query, key, value, segment_row))
    attended = dense(context_rows, output_weight) + output_bias.astype(jnp.float32)
    first_sum = flattened.astype(jnp.float32) + attended
    first_norm, first_back = jax.vjp(
        layer_norm, first_sum, first_gain.astype(jnp.float32), first_shift.astype(jnp.float32)
    )
    norm_low = first_norm.astype(jnp.bfloat16)
    inner = dense(norm_low, inner_weight) + inner_bias.astype(jnp.float32)
    activation, gelu_back = jax.vjp(gelu_exact, inner)
    act_low = activation.astype(jnp.bfloat16)
    outer = dense(act_low, outer_weight) + outer_bias.astype(jnp.float32)
    second_sum = first_norm + outer
    result, second_back = jax.vjp(
        layer_norm, second_sum, second_gain.astype(jnp.float32), second_shift.astype(jnp.float32)
    )
    layer_out = own_halves(result.astype(jnp.bfloat16))
    grad_second, second_gain_term, second_shift_term = second_back(grad_result)
    grad_outer = grad_second.astype(jnp.bfloat16)
    outer_weight_term = dense(act_low.T, grad_outer)
    outer_weight_grad = scatter_sum(outer_weight_term, (0, 1, 2, 3))
    outer_bias_term = jnp.sum(grad_outer.astype(jnp.float32), axis=0)
    (grad_inner_full,) = gelu_back(dense(grad_outer, outer_weight.T))
    grad_inner = grad_inner_full.astype(jnp.bfloat16)
    inner_weight_term = dense(norm_low.T, grad_inner)
    inner_weight_grad = scatter_sum(inner_weight_term, (1, 2, 0, 3))
    inner_bias_term = jnp.sum(grad_inner.astype(jnp.float32), axis=0)
    grad_norm = grad_second + dense(grad_inner, inner_weight.T)
    grad_first, first_gain_term, first_shift_term = first_back(grad_norm)
    grad_attn = grad_first.astype(jnp.bfloat16)
    output_weight_term = dense(context_rows.T, grad_attn)
    output_bias_term = jnp.sum(grad_attn.astype(jnp.float32), axis=0)
    grad_context = dense(grad_attn, output_weight.T).astype(jnp.bfloat16)
    grad_query, grad_key, grad_value = attend_backward(
        (query, key, value, segment_row, grad_context, logsum)
    )
    query_weight_term = dense(flattened.T, grad_query)
    query_bias_term = jnp.sum(grad_query.astype(jnp.float32), axis=0)
    key_weight_term = dense(flattened.T, grad_key)
    value_weight_term = dense(flattened.T, grad_value)
    value_bias_term = jnp.sum(grad_value.astype(jnp.float32), axis=0)
    tokens_grad = (
        grad_first
        + dense(grad_query, query_weight.T)
        + dense(grad_key, key_weight.T)
        + dense(grad_value, value_weight.T)
    )
    tokens_grad = own_halves(tokens_grad.astype(jnp.bfloat16))
    vectors = [
        query_bias_term,
        value_bias_term,
        output_bias_term,
        first_gain_term,
        first_shift_term,
        inner_bias_term,
        outer_bias_term,
        second_gain_term,
        second_shift_term,
    ]
    packed = jnp.concatenate([v.reshape(size, -1) for v in vectors], axis=1)
    wide = packed.shape[1]
    pad = -wide % 256
    packed = jnp.pad(packed, ((0, 0), (0, pad))).reshape(size * 2, (wide + pad) // 2)
    packed_grad = scatter_sum(packed, (2, 0, 1, 3)).reshape(-1)
    vector_grads = []
    at = 0
    for v in vectors:
        step = v.shape[0] // size
        vector_grads.append(packed_grad[at : at + step])
        at += step
    output_weight_grad = scatter_sum(output_weight_term, (2, 0, 1, 3))
    query_weight_grad = scatter_sum(query_weight_term, (0, 1, 2, 3))
    key_weight_grad = scatter_sum(key_weight_term, (1, 2, 0, 3))
    value_weight_grad = scatter_sum(value_weight_term, (2, 0, 1, 3))
    (
        query_bias_grad,
        value_bias_grad,
        output_bias_grad,
        first_gain_grad,
        first_shift_grad,
        inner_bias_grad,
        outer_bias_grad,
        second_gain_grad,
        second_shift_grad,
    ) = vector_grads
    return (
        layer_out,
        tokens_grad,
        query_weight_grad,
        query_bias_grad,
        key_weight_grad,
        value_weight_grad,
        value_bias_grad,
        output_weight_grad,
        output_bias_grad,
        first_gain_grad,
        first_shift_grad,
        inner_weight_grad,
        inner_bias_grad,
        outer_weight_grad,
        outer_bias_grad,
        second_gain_grad,
        second_shift_grad,
    )


def solution(mesh):
    split = P("dp", "seq", None)
    return jax.shard_map(
        shards,
        mesh=mesh,
        in_specs=(split, P("dp", None)) + (P(),) * 15 + (split,),
        out_specs=(
            split,
            split,
            P("dp", None),
            P("dp"),
            P("dp", None),
            P("dp", None),
            P("dp"),
            P("dp", None),
            P("dp"),
            P("dp"),
            P("dp"),
            P("dp", None),
            P("dp"),
            P("dp", None),
            P("dp"),
            P("dp"),
            P("dp"),
        ),
        check_vma=False,
    )
```

time: 1270 us -> 523 us (0.41)
  waiting for transfers between devices: 668 us -> 55.9 us
  blocking collectives: 103 us -> 0 us
  local copies, waits for them, and re-layouts: 125 us -> 35.7 us
  other arithmetic: 87.9 us -> 118 us
  starting transfers between devices: 17.1 us -> 46.2 us
  between operations: 16.5 us -> 2.79 us
    reduce_scatter x3 -> x0, waiting for transfers between devices: 349 us -> none  [the longest x1 174 us: shards(): lax.psum_scatter(outer_weight_term, 'dp', scatter_dimension=0, tiled=True)]
    unnamed x10 -> x0, waiting for transfers between devices: 317 us -> none
    unnamed x1 -> x0, blocking collectives: 75.3 us -> none
    ppermute x0 -> x46, waiting for transfers between devices: none -> 55.9 us  [the longest x28 55.2 us: scatter_sum(): got = lax.ppermute(sent, 'dp', [(i, i ^ 1 << bit) for i in range(size)])]
    ppermute x0 -> x46, starting transfers between devices: none -> 46.2 us  [the longest x28 42.3 us: scatter_sum(): got = lax.ppermute(sent, 'dp', [(i, i ^ 1 << bit) for i in range(size)])]
    all_to_all x12 -> x0, local copies, waits for them, and re-layouts: 33.6 us -> none  [the longest x2 7.99 us: shards(): lax.all_to_all(value, 'seq', split_axis=2, concat_axis=1, tiled=True)]
    while x64 -> x0, local copies, waits for them, and re-layouts: 25.3 us -> none  [the longest x3 15 us: shards(): lax.map(attend_backward, (heads_query, heads_key, heads_value, segments,...]
    all_to_all x4 -> x0, blocking collectives: 25.2 us -> none  [the longest x1 6.58 us: shards(): lax.all_to_all(for_sending(context), 'seq', split_axis=1, concat_axis=2,...]
  transfers between devices with their start and end apart: 11 -> 46, of which waited for: 6 -> 14; matrix products, arithmetic and copies ran while one was open for 21% -> 40% of each run, Pallas kernels for 0% -> 0%
where the time goes in v1:
time: 523 us; the launch traced here: 512 us
  matrix products  254 us (49%)
  other arithmetic  118 us (23%)
  waiting for transfers between devices  55.9 us (11%)
  starting transfers between devices  46.2 us (9%)
  local copies, waits for them, and re-layouts  35.7 us (7%)
    dot_general x18, matrix products, dense(): return jnp.dot(left, right, preferred_element_type=jnp.float32)  114 us
    ppermute x28, waiting for transfers between devices, scatter_sum(): got = lax.ppermute(sent, 'dp', [(i, i ^ 1 << bit) for i in range(size)])  55.2 us
    convert_element_type x2, other arithmetic, attend_backward(): grad_scores = (probs * (grad_probs - inner)).astype(jnp.bfloat16)  43.4 us
    ppermute x28, starting transfers between devices, scatter_sum(): got = lax.ppermute(sent, 'dp', [(i, i ^ 1 << bit) for i in range(size)])  42.3 us
    dot_general x2, matrix products, attend_backward(): jnp.einsum('qhd,khd->hqk', grad_block, heads_value, preferred_element_typ...  36.1 us
    dot_general x2, matrix products, attend_backward(): jnp.einsum('hqk,qhd->khd', probs_low, grad_block, preferred_element_type=...  26.7 us
    reduce_sum x2, other arithmetic, attend_forward(): total = jnp.sum(weights, axis=-1)  24.4 us
    dot_general x2, matrix products, attend_forward(): jnp.einsum('hqk,khd->qhd', probs, heads_value, preferred_element_type=jnp...  22.8 us
  transfers between devices with their start and end apart: 46, of which 14 were waited for; matrix products, arithmetic and copies ran while one was open for 40% of the time, Pallas kernels for 0%

profile of v1, /device:TPU:0, one launch (start us, length us, event | category | flops | bytes accessed | tf_op | source)
XLA Modules:
  0.0 512.4 jit_solution(7848752356110347609)
XLA Ops:
  0.8 2.2 dynamic-slice_bitcast_fusion.1
  9.8 3.3 add_convert_fusion.4
  17.7 10.5 %select_reduce_fusion.1 = (f32[12,512]{1,0:T(8,128)S(1)}, f32[12,512,1024]{2,1,0:T(8,128)}) fusion(pred[512,1024]{1,0:T(8,128)(4,1)S(1)} %get-tuple-element.70, bf16[512,12,64]{0,2,1:T(8,128)(2,1)S(1)} %bitcast.708, bf16[1024,12,64]{0,2,1:T(8,128)(2,1)S(1)} %bitcast.702), kind=kOutput, calls=%fused_computation.11 | convolution fusion | flops 824174592 | bytes 28073984 | tf_op jit(solution)/shard_map/qhd,khd->hqk/dot_general | solution.py:34
  28.3 12.1 %fusion = f32[12,512]{1,0:T(8,128)S(1)} fusion(f32[12,512,1024]{2,1,0:T(8,128)} %get-tuple-element.85, f32[12,512]{1,0:T(8,128)S(1)} %broadcast_select_fusion.15, pred[512,1024]{1,0:T(8,128)(4,1)S(1)} %get-tuple-element.70), kind=kLoop, calls=%fused_computation.12 | loop fusion | flops 25159680 | bytes 25739264 | tf_op jit(solution)/shard_map/reduce_sum | solution.py:60
  40.4 10.6 %select_reduce_fusion = (f32[12,512]{1,0:T(8,128)S(1)}, f32[12,512,1024]{2,1,0:T(8,128)}) fusion(pred[512,1024]{1,0:T(8,128)(4,1)S(1)} %get-tuple-element.71, bf16[512,12,64]{0,2,1:T(8,128)(2,1)S(1)} %bitcast.706, bf16[1024,12,64]{0,2,1:T(8,128)(2,1)S(1)} %bitcast.703), kind=kOutput, calls=%fused_computation.8 | convolution fusion | flops 824174592 | bytes 28073984 | tf_op jit(solution)/shard_map/qhd,khd->hqk/dot_general | solution.py:34
  50.9 12.3 %fusion.1 = f32[12,512]{1,0:T(8,128)S(1)} fusion(f32[12,512,1024]{2,1,0:T(8,128)} %get-tuple-element.83, f32[12,512]{1,0:T(8,128)S(1)} %broadcast_select_fusion.14, pred[512,1024]{1,0:T(8,128)(4,1)S(1)} %get-tuple-element.71), kind=kLoop, calls=%fused_computation.13 | loop fusion | flops 25159680 | bytes 25739264 | tf_op jit(solution)/shard_map/reduce_sum | solution.py:60
  64.0 14.1 %fusion.29 = bf16[12,64,512]{2,1,0:T(8,128)(2,1)} fusion(bf16[1024,12,64]{0,2,1:T(8,128)(2,1)S(1)} %bitcast.710, f32[12,512,1024]{2,1,0:T(8,128)} %get-tuple-element.83, f32[12,512]{1,0:T(8,128)S(1)} %get-tuple-element.28, f32[12,512]{1,0:T(8,128)S(1)} %broadcast_select_fusion.14, pred[512,1024]{1,0:T(8,128)(4,1)S(1)} %get-tuple-element.71), kind=kOutput, calls=%fused_computation.90 | convolution fusion | flops 837156864 | bytes 28098560 | tf_op jit(solution)/shard_map/hqk,khd->qhd/dot_general | solution.py:63
  78.3 8.7 %fusion.30 = bf16[12,64,512]{2,1,0:T(8,128)(2,1)} fusion(bf16[1024,12,64]{0,2,1:T(8,128)(2,1)S(1)} %bitcast.711, f32[12,512,1024]{2,1,0:T(8,128)S(1)} %bitcast.693, f32[12,512]{1,0:T(8,128)S(1)} %get-tuple-element.101, f32[12,512]{1,0:T(8,128)S(1)} %broadcast_select_fusion.15, pred[512,1024]{1,0:T(8,128)(4,1)S(1)} %get-tuple-element.70), kind=kOutput, calls=%fused_computation.91 | convolution fusion | flops 837156864 | bytes 28098560 | tf_op jit(solution)/shard_map/hqk,khd->qhd/dot_general | solution.py:63
  87.0 3.4 fusion.171
  91.1 35.4 %multiply_convert_fusion.2 = (bf16[1024,3072]{1,0:T(8,128)(2,1)S(1)}, f32[1024,3072]{1,0:T(8,128)}, f32[1024,3072]{1,0:T(8,128)}) fusion(f32[3072]{0:T(1024)S(1)} %convert_element_type.1066, bf16[768,3072]{1,0:T(8,128)(2,1)S(1)} %bitcast.763, f32[1024,768]{1,0:T(8,128)S(1)} %get-tuple-element.87, f32[768]{0:T(1024)S(1)} %convert_element_type.1064, ...), kind=kOutput, calls=%fused_computation.20 | convolution fusion | flops 5043388416 | bytes 39348224 | tf_op jit(solution)/shard_map/dot_general | solution.py:22
  126.6 5.5 %fusion.172 = (f32[1024]{0:T(1024)S(1)}, f32[1024,768]{1,0:T(8,128)S(1)}) fusion(f32[768]{0:T(1024)S(1)} %copy-done.49, bf16[1024,3072]{1,0:T(8,128)(2,1)S(1)} %get-tuple-element.35, bf16[3072,768]{1,0:T(8,128)(2,1)S(1)} %bitcast.761, f32[768]{0:T(1024)S(1)} %convert_element_type.1064, f32[768]{0:T(1024)S(1)} %convert_element_type.1063, ...), kind=kOutput, calls=%fused_computation.452 | convolution fusion | flops 4837342208 | bytes 17323008 | tf_op jit(solution)/shard_map/dot_general | solution.py:22
  135.3 3.0 fusion.21
  138.3 3.2 fusion.166
  144.1 16.7 %convert_reduce_fusion = (f32[3072]{0:T(1024)S(1)}, bf16[1024,3072]{1,0:T(8,128)(2,1)}) fusion(f32[1024,3072]{1,0:T(8,128)} %get-tuple-element.36, bf16[1024,768]{1,0:T(8,128)(2,1)S(1)} %get-tuple-element.24, bf16[3072,768]{1,0:T(8,128)(2,1)} %param.31, f32[1024,3072]{1,0:T(8,128)} %get-tuple-element.88, f32[3072]{0:T(1024)S(1)} %convert_element_type.1066), kind=kOutput, calls=%fused_computation.18 | convolution fusion | flops 4885312512 | bytes 37773312 | tf_op jit(solution)/shard_map/dot_general | solution.py:22
  160.9 10.3 %multiply_reduce_fusion.2 = (f32[768]{0:T(1024)S(1)}, f32[1024]{0:T(1024)S(1)}, f32[768]{0:T(1024)S(1)}, f32[1024,768]{1,0:T(8,128)S(1)}) fusion(f32[1024,768]{1,0:T(8,128)S(1)} %get-tuple-element.87, f32[1024]{0:T(1024)S(1)} %fusion.106, f32[1024]{0:T(1024)S(1)} %broadcast_multiply_fusion.1, f32[768]{0:T(1024)S(1)} %convert_element_type.1063, ...), kind=kOutput, calls=%fused_computation.52 | convolution fusion | flops 4839699456 | bytes 20472832 | tf_op jit(solution)/shard_map/dot_general | solution.py:22
  171.2 8.4 %fusion.161 = f32[768,3072]{1,0:T(8,128)} fusion(bf16[1024,3072]{1,0:T(8,128)(2,1)S(1)} %copy-done.15, f32[1024,768]{1,0:T(8,128)S(1)} %get-tuple-element.87, f32[768]{0:T(1024)S(1)} %convert_element_type.1064, f32[768]{0:T(1024)S(1)} %convert_element_type.1063, f32[1024]{0:T(1024)S(1)} %fusion.106, f32[1024]{0:T(1024)S(1)} %broadcast_multiply_fusion.1), kind=kOutput, calls=%fused_computation.444 | convolution fusion | flops 4835770368 | bytes 18888704 | tf_op jit(solution)/shard_map/dot_general | solution.py:22
  183.7 2.8 fusion.33
  188.0 7.7 %fusion.177 = f32[3072,768]{1,0:T(8,128)} fusion(bf16[1024,3072]{1,0:T(8,128)(2,1)S(1)} %bitcast.769, bf16[1024,768]{1,0:T(8,128)(2,1)S(1)} %get-tuple-element.24), kind=kOutput, calls=%fused_computation.457 | convolution fusion | flops 4831838208 | bytes 17301504 | tf_op jit(solution)/shard_map/dot_general | solution.py:22
  197.8 17.9 %multiply_reduce_fusion.1 = (f32[12,512]{1,0:T(8,128)S(1)}, f32[12,512,1024]{2,1,0:T(8,128)}) fusion(f32[12,512,1024]{2,1,0:T(8,128)} %get-tuple-element.85, f32[12,512]{1,0:T(8,128)S(1)} %copy-done.37, pred[512,1024]{1,0:T(8,128)(4,1)S(1)} %copy-done.7, bf16[512,12,64]{0,2,1:T(8,128)(2,1)} %bitcast.734, bf16[1024,12,64]{0,2,1:T(8,128)(2,1)S(1)} %bitcast.713), kind=kOutput, calls=%fused_computation.4 | convolution fusion | flops 836757504 | bytes 53264384 | tf_op jit(solution)/shard_map/qhd,khd->hqk/dot_general | solution.py:90
  215.7 21.3 %multiply_convert_fusion.1 = bf16[12,512,1024]{2,1,0:T(8,128)(2,1)} fusion(f32[12,512,1024]{2,1,0:T(8,128)} %get-tuple-element.93, f32[12,512,1024]{2,1,0:T(8,128)} %get-tuple-element.85, f32[12,512]{1,0:T(8,128)S(1)} %get-tuple-element.92, f32[12,512]{1,0:T(8,128)S(1)} %copy-done.37, pred[512,1024]{1,0:T(8,128)(4,1)S(1)} %copy-done.7), kind=kLoop, calls=%fused_computation.3 | loop fusion | flops 37748736 | bytes 63488000 | tf_op jit(solution)/shard_map/convert_element_type | solution.py:97
  237.0 9.5 %multiply_convert_fusion.5 = bf16[12,64,512]{2,1,0:T(8,128)(2,1)} fusion(bf16[1024,12,64]{0,2,1:T(8,128)(2,1)S(1)} %bitcast.704, bf16[12,512,1024]{2,1,0:T(8,128)(2,1)} %multiply_convert_fusion.1), kind=kOutput, calls=%fused_computation.89 | convolution fusion | flops 806092800 | bytes 14942208 | tf_op jit(solution)/shard_map/hqk,khd->qhd/dot_general | solution.py:99
  246.5 8.7 %fusion.173 = f32[12,64,1024]{2,1,0:T(8,128)} fusion(bf16[512,12,64]{0,2,1:T(8,128)(2,1)S(1)} %bitcast.709, bf16[12,512,1024]{2,1,0:T(8,128)(2,1)} %multiply_convert_fusion.1), kind=kOutput, calls=%fused_computation.453 | convolution fusion | flops 805306368 | bytes 16515072 | tf_op jit(solution)/shard_map/hqk,qhd->khd/dot_general | solution.py:105
  255.2 13.6 %fusion.10 = f32[12,64,1024]{2,1,0:T(8,128)} fusion(bf16[512,12,64]{0,2,1:T(8,128)(2,1)S(1)} %bitcast.737, f32[12,512,1024]{2,1,0:T(8,128)} %get-tuple-element.83, f32[12,512]{1,0:T(8,128)S(1)} %copy-done.38, pred[512,1024]{1,0:T(8,128)(4,1)S(1)} %copy-done.9), kind=kOutput, calls=%fused_computation.33 | convolution fusion | flops 830472192 | bytes 29646848 | tf_op jit(solution)/shard_map/hqk,qhd->khd/dot_general | solution.py:93
  268.8 18.2 %multiply_reduce_fusion = (f32[12,512]{1,0:T(8,128)S(1)}, f32[12,512,1024]{2,1,0:T(8,128)}) fusion(f32[12,512,1024]{2,1,0:T(8,128)} %get-tuple-element.83, f32[12,512]{1,0:T(8,128)S(1)} %copy-done.38, pred[512,1024]{1,0:T(8,128)(4,1)} %copy-done.8, bf16[512,12,64]{0,2,1:T(8,128)(2,1)} %bitcast.736, bf16[1024,12,64]{0,2,1:T(8,128)(2,1)} %bitcast.712), kind=kOutput, calls=%fused_computation.1 | convolution fusion | flops 836757504 | bytes 53264384 | tf_op jit(solution)/shard_map/qhd,khd->hqk/dot_general | solution.py:90
  286.9 22.1 %multiply_convert_fusion = bf16[12,512,1024]{2,1,0:T(8,128)(2,1)} fusion(f32[12,512,1024]{2,1,0:T(8,128)} %get-tuple-element.95, f32[12,512,1024]{2,1,0:T(8,128)} %get-tuple-element.83, f32[12,512]{1,0:T(8,128)S(1)} %get-tuple-element.94, f32[12,512]{1,0:T(8,128)S(1)} %copy-done.38, pred[512,1024]{1,0:T(8,128)(4,1)} %copy-done.8), kind=kLoop, calls=%fused_computation | loop fusion | flops 37748736 | bytes 63488000 | tf_op jit(solution)/shard_map/convert_element_type | solution.py:97
  309.1 8.6 %multiply_convert_fusion.4 = bf16[12,64,512]{2,1,0:T(8,128)(2,1)S(1)} fusion(bf16[1024,12,64]{0,2,1:T(8,128)(2,1)S(1)} %bitcast.705, bf16[12,512,1024]{2,1,0:T(8,128)(2,1)} %multiply_convert_fusion), kind=kOutput, calls=%fused_computation.88 | convolution fusion | flops 806092800 | bytes 14942208 | tf_op jit(solution)/shard_map/hqk,khd->qhd/dot_general | solution.py:99
  318.0 2.8 fusion.48
  320.8 3.1 fusion.49
  328.6 2.3 fusion.41
  331.0 4.0 fusion.23
  335.1 13.2 %convert_reduce_fusion.4 = (f32[12,64]{1,0:T(8,128)S(1)}, bf16[12,64,1024]{2,1,0:T(8,128)(2,1)}) fusion(f32[12,64,1024]{2,1,0:T(8,128)S(1)} %copy-done.63, bf16[512,12,64]{0,2,1:T(8,128)(2,1)S(1)} %bitcast.735, f32[12,512,1024]{2,1,0:T(8,128)} %get-tuple-element.85, f32[12,512]{1,0:T(8,128)S(1)} %copy-done.37, pred[512,1024]{1,0:T(8,128)(4,1)S(1)} %copy-done.7), kind=kOutput, calls=%fused_computation.54 | convolution fusion | flops 833617152 | bytes 31222784 | tf_op jit(solution)/shard_map/hqk,qhd->khd/dot_general | solution.py:93
  348.3 3.5 fusion.176
  353.8 6.9 %multiply_convert_fusion.3 = bf16[12,64,1024]{2,1,0:T(8,128)(2,1)S(1)} fusion(f32[12,64,1024]{2,1,0:T(8,128)S(1)} %copy-done.3, bf16[512,12,64]{0,2,1:T(8,128)(2,1)S(1)} %bitcast.707, bf16[12,512,1024]{2,1,0:T(8,128)(2,1)} %multiply_convert_fusion), kind=kOutput, calls=%fused_computation.58 | convolution fusion | flops 807665664 | bytes 18087936 | tf_op jit(solution)/shard_map/hqk,qhd->khd/dot_general | solution.py:105
  361.2 2.9 fusion.175
  370.7 3.0 collective-permute-start.11
  377.3 4.1 fusion.24
  385.1 2.6 collective-permute-start.14
  390.4 2.2 fusion.39
  410.7 4.5 collective-permute-done.23
  432.5 2.6 collective-permute-start.32
  437.3 2.7 collective-permute-start.20
  449.8 21.3 %collective-permute-done.35 = bf16[2,2,2,24,3072]{4,3,2,1,0:T(8,128)(2,1)S(1)} collective-permute-done((bf16[2,2,2,24,3072]{4,3,2,1,0:T(8,128)(2,1)S(1)}, bf16[2,2,2,24,3072]{4,3,2,1,0:T(8,128)(2,1)S(1)}, u32[]{:S(2)}, u32[]{:S(2)}) %collective-permute-start.35) | collective-permute-done | bytes 1179680 | tf_op jit(solution)/shard_map/ppermute | solution.py:143
  476.9 9.3 %collective-permute-done.36 = bf16[2,2,24,3072]{3,2,1,0:T(8,128)(2,1)S(1)} collective-permute-done((bf16[2,2,24,3072]{3,2,1,0:T(8,128)(2,1)S(1)}, bf16[2,2,24,3072]{3,2,1,0:T(8,128)(2,1)S(1)}, u32[]{:S(2)}, u32[]{:S(2)}) %collective-permute-start.36) | collective-permute-done | bytes 589856 | tf_op jit(solution)/shard_map/ppermute | solution.py:143
  491.2 3.2 collective-permute-done.37
  494.5 2.7 collective-permute-start.38
  497.8 2.1 collective-permute-done.43
  500.0 2.9 collective-permute-start.44
  502.9 4.7 collective-permute-done.38
  (384 shorter events, 112.9 us)
Async XLA Ops:
  0.7 86.3 %copy-start = (bf16[768,768]{1,0:T(8,128)(2,1)S(1)}, bf16[768,768]{1,0:T(8,128)(2,1)}, u32[]{:S(2)}) copy-start(bf16[768,768]{1,0:T(8,128)(2,1)} %param.25) | copy-start | bytes 3538948
  3.0 130.9 %collective-permute-start.2 = (bf16[512,768]{1,0:T(8,128)(2,1)}, bf16[512,768]{1,0:T(8,128)(2,1)}, u32[]{:S(2)}, u32[]{:S(2)}) collective-permute-start(bf16[512,768]{1,0:T(8,128)(2,1)} %dynamic-slice_bitcast_fusion.1), channel_id=1, source_target_pairs={{0,1},{1,0},{2,3},{3,2},{4,5},{5,4},{6,7},{7,6},{8,9},{9,8},{10,11... | collective-permute-start | bytes 2359304 | tf_op jit(solution)/shard_map/ppermute | solution.py:179
  4.6 3.3 collective-permute-start
  9.8 122.2 %copy-start.22 = (bf16[512,768]{1,0:T(8,128)(2,1)}, bf16[512,768]{1,0:T(8,128)(2,1)S(1)}, u32[]{:S(2)}) copy-start(bf16[512,768]{1,0:T(8,128)(2,1)S(1)} %get-tuple-element.50) | copy-start | bytes 2359300
  327.8 74.3 %collective-permute-start.1 = (bf16[512,768]{1,0:T(8,128)(2,1)}, bf16[512,768]{1,0:T(8,128)(2,1)}, u32[]{:S(2)}, u32[]{:S(2)}) collective-permute-start(bf16[512,768]{1,0:T(8,128)(2,1)} %dynamic-slice_bitcast_fusion.2), channel_id=1, source_target_pairs={{0,1},{1,0},{2,3},{3,2},{4,5},{5,4},{6,7},{7,6},{8,9},{9,8},{10,11... | collective-permute-start | bytes 2359304 | tf_op jit(solution)/shard_map/ppermute | solution.py:187
  330.9 62.2 %collective-permute-start.28 = (bf16[2,2,2,2,24,768]{5,4,0,3,2,1:T(8,128)(2,1)}, bf16[2,2,2,2,24,768]{5,4,0,3,2,1:T(8,128)(2,1)}, u32[]{:S(2)}, u32[]{:S(2)}) collective-permute-start(bf16[2,2,2,2,24,768]{5,4,0,3,2,1:T(8,128)(2,1)} %fusion.41), channel_id=1, source_target_pairs={{0,1},{1,0},{2,3},{3,2},{4,5},{5,4},{6,7},{7,6},{8,9},{9,8},{10,11... | collective-permute-start | bytes 1769480 | tf_op jit(solution)/shard_map/ppermute | solution.py:137
  353.4 42.5 %collective-permute-start.22 = (bf16[2,2,2,2,24,768]{5,4,0,3,2,1:T(8,128)(2,1)}, bf16[2,2,2,2,24,768]{5,4,0,3,2,1:T(8,128)(2,1)}, u32[]{:S(2)}, u32[]{:S(2)}) collective-permute-start(bf16[2,2,2,2,24,768]{5,4,0,3,2,1:T(8,128)(2,1)} %fusion.40), channel_id=1, source_target_pairs={{0,1},{1,0},{2,3},{3,2},{4,5},{5,4},{6,7},{7,6},{8,9},{9,8},{10,11... | collective-permute-start | bytes 1769480 | tf_op jit(solution)/shard_map/ppermute | solution.py:137
  361.0 9.6 %collective-permute-start.10 = (bf16[2,2,2,2,1,384]{5,3,2,1,0,4:T(2,128)(2,1)S(1)}, bf16[2,2,2,2,1,384]{5,3,2,1,0,4:T(2,128)(2,1)S(1)}, u32[]{:S(2)}, u32[]{:S(2)}) collective-permute-start(bf16[2,2,2,2,1,384]{5,3,2,1,0,4:T(2,128)(2,1)S(1)} %bitcast.759), channel_id=1, source_target_pairs={{0,1},{1,0},{2,3},{3,2},{4,5},{5,4},{6,7},{7,6},{8,9},{9,8},{10,11... | collective-permute-start | bytes 36872 | tf_op jit(solution)/shard_map/ppermute | solution.py:137
  370.7 4.6 collective-permute-start.11
  375.3 6.1 %collective-permute-start.12 = (bf16[2,2,1,384]{3,1,2,0:T(2,128)(2,1)S(1)}, bf16[2,2,1,384]{3,1,2,0:T(2,128)(2,1)S(1)}, u32[]{:S(2)}, u32[]{:S(2)}) collective-permute-start(bf16[2,2,1,384]{3,1,2,0:T(2,128)(2,1)S(1)} %fusion.105), channel_id=1, source_target_pairs={{0,2},{2,0},{4,6},{6,4},{8,10},{10,8},{12,14},{14,12},{16,18},{18,... | collective-permute-start | bytes 9224 | tf_op jit(solution)/shard_map/ppermute | solution.py:143
  381.4 3.7 collective-permute-start.13
  383.9 15.5 %collective-permute-start.16 = (bf16[2,2,2,2,24,768]{5,4,3,2,1,0:T(8,128)(2,1)}, bf16[2,2,2,2,24,768]{5,4,3,2,1,0:T(8,128)(2,1)}, u32[]{:S(2)}, u32[]{:S(2)}) collective-permute-start(bf16[2,2,2,2,24,768]{5,4,3,2,1,0:T(8,128)(2,1)} %fusion.38), channel_id=1, source_target_pairs={{0,1},{1,0},{2,3},{3,2},{4,5},{5,4},{6,7},{7,6},{8,9},{9,8},{10,11... | collective-permute-start | bytes 1769480 | tf_op jit(solution)/shard_map/ppermute | solution.py:137
  385.1 4.5 collective-permute-start.14
  390.4 2.2 collective-permute-start.15
  392.6 5.3 %collective-permute-start.4 = (bf16[2,2,2,2,24,768]{5,4,0,3,2,1:T(8,128)(2,1)}, bf16[2,2,2,2,24,768]{5,4,0,3,2,1:T(8,128)(2,1)}, u32[]{:S(2)}, u32[]{:S(2)}) collective-permute-start(bf16[2,2,2,2,24,768]{5,4,0,3,2,1:T(8,128)(2,1)} %fusion.39), channel_id=1, source_target_pairs={{0,1},{1,0},{2,3},{3,2},{4,5},{5,4},{6,7},{7,6},{8,9},{9,8},{10,11... | collective-permute-start | bytes 1769480 | tf_op jit(solution)/shard_map/ppermute | solution.py:137
  393.1 10.8 %collective-permute-start.3 = (bf16[512,768]{1,0:T(8,128)(2,1)S(1)}, bf16[512,768]{1,0:T(8,128)(2,1)S(1)}, u32[]{:S(2)}, u32[]{:S(2)}) collective-permute-start(bf16[512,768]{1,0:T(8,128)(2,1)S(1)} %dynamic-slice_bitcast_fusion), channel_id=1, source_target_pairs={{0,1},{1,0},{2,3},{3,2},{4,5},{5,4},{6,7},{7,6},{8,9},{9,8},{10,11... | collective-permute-start | bytes 2359304 | tf_op jit(solution)/shard_map/ppermute | solution.py:187
  395.9 46.3 %collective-permute-start.34 = (bf16[2,2,2,2,24,3072]{5,4,0,3,2,1:T(8,128)(2,1)}, bf16[2,2,2,2,24,3072]{5,4,0,3,2,1:T(8,128)(2,1)S(1)}, u32[]{:S(2)}, u32[]{:S(2)}) collective-permute-start(bf16[2,2,2,2,24,3072]{5,4,0,3,2,1:T(8,128)(2,1)} %fusion.23), channel_id=1, source_target_pairs={{0,1},{1,0},{2,3},{3,2},{4,5},{5,4},{6,7},{7,6},{8,9},{9,8},{10,11... | collective-permute-start | bytes 7077896 | tf_op jit(solution)/shard_map/ppermute | solution.py:137
  397.9 48.1 %collective-permute-start.40 = (bf16[2,2,2,2,96,768]{5,4,0,3,2,1:T(8,128)(2,1)S(1)}, bf16[2,2,2,2,96,768]{5,4,0,3,2,1:T(8,128)(2,1)S(1)}, u32[]{:S(2)}, u32[]{:S(2)}) collective-permute-start(bf16[2,2,2,2,96,768]{5,4,0,3,2,1:T(8,128)(2,1)S(1)} %copy-done.29), channel_id=1, source_target_pairs={{0,1},{1,0},{2,3},{3,2},{4,5},{5,4},{6,7},{7,6},{8,9},{9,8},{10,11... | collective-permute-start | bytes 7077896 | tf_op jit(solution)/shard_map/ppermute | solution.py:137
  399.4 9.9 %collective-permute-start.29 = (bf16[2,2,2,24,768]{4,3,2,1,0:T(8,128)(2,1)S(1)}, bf16[2,2,2,24,768]{4,3,2,1,0:T(8,128)(2,1)S(1)}, u32[]{:S(2)}, u32[]{:S(2)}) collective-permute-start(bf16[2,2,2,24,768]{4,3,2,1,0:T(8,128)(2,1)S(1)} %copy.149), channel_id=1, source_target_pairs={{0,8},{2,10},{4,12},{6,14},{8,0},{10,2},{12,4},{14,6},{16,24},{18,... | collective-permute-start | bytes 884744 | tf_op jit(solution)/shard_map/ppermute | solution.py:143
  402.1 13.1 %collective-permute-start.23 = (bf16[2,2,2,24,768]{4,3,2,1,0:T(8,128)(2,1)S(1)}, bf16[2,2,2,24,768]{4,3,2,1,0:T(8,128)(2,1)S(1)}, u32[]{:S(2)}, u32[]{:S(2)}) collective-permute-start(bf16[2,2,2,24,768]{4,3,2,1,0:T(8,128)(2,1)S(1)} %copy.142), channel_id=1, source_target_pairs={{0,8},{2,10},{4,12},{6,14},{8,0},{10,2},{12,4},{14,6},{16,24},{18,... | collective-permute-start | bytes 884744 | tf_op jit(solution)/shard_map/ppermute | solution.py:143
  403.9 12.8 %collective-permute-start.17 = (bf16[2,2,2,24,768]{4,3,2,1,0:T(8,128)(2,1)S(1)}, bf16[2,2,2,24,768]{4,3,2,1,0:T(8,128)(2,1)S(1)}, u32[]{:S(2)}, u32[]{:S(2)}) collective-permute-start(bf16[2,2,2,24,768]{4,3,2,1,0:T(8,128)(2,1)S(1)} %fusion.46), channel_id=1, source_target_pairs={{0,4},{2,6},{4,0},{6,2},{8,12},{10,14},{12,8},{14,10},{16,20},{18,... | collective-permute-start | bytes 884744 | tf_op jit(solution)/shard_map/ppermute | solution.py:143
  409.4 10.0 %collective-permute-start.5 = (bf16[2,2,2,24,768]{4,3,2,1,0:T(8,128)(2,1)S(1)}, bf16[2,2,2,24,768]{4,3,2,1,0:T(8,128)(2,1)S(1)}, u32[]{:S(2)}, u32[]{:S(2)}) collective-permute-start(bf16[2,2,2,24,768]{4,3,2,1,0:T(8,128)(2,1)S(1)} %copy.125), channel_id=1, source_target_pairs={{0,2},{2,0},{4,6},{6,4},{8,10},{10,8},{12,14},{14,12},{16,18},{18,... | collective-permute-start | bytes 884744 | tf_op jit(solution)/shard_map/ppermute | solution.py:143
  415.2 7.0 %collective-permute-start.30 = (bf16[2,2,24,768]{3,2,1,0:T(8,128)(2,1)S(1)}, bf16[2,2,24,768]{3,2,1,0:T(8,128)(2,1)S(1)}, u32[]{:S(2)}, u32[]{:S(2)}) collective-permute-start(bf16[2,2,24,768]{3,2,1,0:T(8,128)(2,1)S(1)} %copy.152), channel_id=1, source_target_pairs={{0,2},{2,0},{4,6},{6,4},{8,10},{10,8},{12,14},{14,12},{16,18},{18,... | collective-permute-start | bytes 442376 | tf_op jit(solution)/shard_map/ppermute | solution.py:143
  416.7 8.1 %collective-permute-start.24 = (bf16[2,2,24,768]{3,2,1,0:T(8,128)(2,1)S(1)}, bf16[2,2,24,768]{3,2,1,0:T(8,128)(2,1)S(1)}, u32[]{:S(2)}, u32[]{:S(2)}) collective-permute-start(bf16[2,2,24,768]{3,2,1,0:T(8,128)(2,1)S(1)} %copy.145), channel_id=1, source_target_pairs={{0,2},{2,0},{4,6},{6,4},{8,10},{10,8},{12,14},{14,12},{16,18},{18,... | collective-permute-start | bytes 442376 | tf_op jit(solution)/shard_map/ppermute | solution.py:143
  419.4 6.9 %collective-permute-start.18 = (bf16[2,2,24,768]{3,2,0,1:T(8,128)(2,1)S(1)}, bf16[2,2,24,768]{3,2,0,1:T(8,128)(2,1)S(1)}, u32[]{:S(2)}, u32[]{:S(2)}) collective-permute-start(bf16[2,2,24,768]{3,2,0,1:T(8,128)(2,1)S(1)} %copy.137), channel_id=1, source_target_pairs={{0,8},{2,10},{4,12},{6,14},{8,0},{10,2},{12,4},{14,6},{16,24},{18,... | collective-permute-start | bytes 442376 | tf_op jit(solution)/shard_map/ppermute | solution.py:143
  422.2 6.7 %collective-permute-start.6 = (bf16[2,2,24,768]{3,2,1,0:T(8,128)(2,1)S(1)}, bf16[2,2,24,768]{3,2,1,0:T(8,128)(2,1)S(1)}, u32[]{:S(2)}, u32[]{:S(2)}) collective-permute-start(bf16[2,2,24,768]{3,2,1,0:T(8,128)(2,1)S(1)} %copy.128), channel_id=1, source_target_pairs={{0,4},{2,6},{4,0},{6,2},{8,12},{10,14},{12,8},{14,10},{16,20},{18,... | collective-permute-start | bytes 442376 | tf_op jit(solution)/shard_map/ppermute | solution.py:143
  424.8 5.7 %collective-permute-start.31 = (bf16[2,24,768]{2,1,0:T(8,128)(2,1)S(1)}, bf16[2,24,768]{2,1,0:T(8,128)(2,1)S(1)}, u32[]{:S(2)}, u32[]{:S(2)}) collective-permute-start(bf16[2,24,768]{2,1,0:T(8,128)(2,1)S(1)} %fusion.58), channel_id=1, source_target_pairs={{0,4},{2,6},{4,0},{6,2},{8,12},{10,14},{12,8},{14,10},{16,20},{18,... | collective-permute-start | bytes 221192 | tf_op jit(solution)/shard_map/ppermute | solution.py:143
  426.4 6.1 %collective-permute-start.25 = (bf16[2,24,768]{2,1,0:T(8,128)(2,1)S(1)}, bf16[2,24,768]{2,1,0:T(8,128)(2,1)S(1)}, u32[]{:S(2)}, u32[]{:S(2)}) collective-permute-start(bf16[2,24,768]{2,1,0:T(8,128)(2,1)S(1)} %fusion.59), channel_id=1, source_target_pairs={{0,4},{2,6},{4,0},{6,2},{8,12},{10,14},{12,8},{14,10},{16,20},{18,... | collective-permute-start | bytes 221192 | tf_op jit(solution)/shard_map/ppermute | solution.py:143
  428.9 7.1 %collective-permute-start.19 = (bf16[2,24,768]{2,1,0:T(8,128)(2,1)S(1)}, bf16[2,24,768]{2,1,0:T(8,128)(2,1)S(1)}, u32[]{:S(2)}, u32[]{:S(2)}) collective-permute-start(bf16[2,24,768]{2,1,0:T(8,128)(2,1)S(1)} %fusion.60), channel_id=1, source_target_pairs={{0,2},{2,0},{4,6},{6,4},{8,10},{10,8},{12,14},{14,12},{16,18},{18,... | collective-permute-start | bytes 221192 | tf_op jit(solution)/shard_map/ppermute | solution.py:143
  430.5 6.8 %collective-permute-start.7 = (bf16[2,24,768]{2,1,0:T(8,128)(2,1)S(1)}, bf16[2,24,768]{2,1,0:T(8,128)(2,1)S(1)}, u32[]{:S(2)}, u32[]{:S(2)}) collective-permute-start(bf16[2,24,768]{2,1,0:T(8,128)(2,1)S(1)} %fusion.61), channel_id=1, source_target_pairs={{0,8},{2,10},{4,12},{6,14},{8,0},{10,2},{12,4},{14,6},{16,24},{18,... | collective-permute-start | bytes 221192 | tf_op jit(solution)/shard_map/ppermute | solution.py:143
  432.5 8.4 %collective-permute-start.32 = (bf16[24,768]{1,0:T(8,128)(2,1)S(1)}, bf16[24,768]{1,0:T(8,128)(2,1)S(1)}, u32[]{:S(2)}, u32[]{:S(2)}) collective-permute-start(bf16[24,768]{1,0:T(8,128)(2,1)S(1)} %fusion.62), channel_id=1, source_target_pairs={{0,16},{2,18},{4,20},{6,22},{8,24},{10,26},{12,28},{14,30},{16,0},... | collective-permute-start | bytes 110600 | tf_op jit(solution)/shard_map/ppermute | solution.py:143
  436.1 6.6 %collective-permute-start.26 = (bf16[24,768]{1,0:T(8,128)(2,1)S(1)}, bf16[24,768]{1,0:T(8,128)(2,1)S(1)}, u32[]{:S(2)}, u32[]{:S(2)}) collective-permute-start(bf16[24,768]{1,0:T(8,128)(2,1)S(1)} %fusion.64), channel_id=1, source_target_pairs={{0,16},{2,18},{4,20},{6,22},{8,24},{10,26},{12,28},{14,30},{16,0},... | collective-permute-start | bytes 110600 | tf_op jit(solution)/shard_map/ppermute | solution.py:143
  437.3 7.7 %collective-permute-start.20 = (bf16[24,768]{1,0:T(8,128)(2,1)S(1)}, bf16[24,768]{1,0:T(8,128)(2,1)S(1)}, u32[]{:S(2)}, u32[]{:S(2)}) collective-permute-start(bf16[24,768]{1,0:T(8,128)(2,1)S(1)} %fusion.66), channel_id=1, source_target_pairs={{0,16},{2,18},{4,20},{6,22},{8,24},{10,26},{12,28},{14,30},{16,0},... | collective-permute-start | bytes 110600 | tf_op jit(solution)/shard_map/ppermute | solution.py:143
  440.8 5.9 %collective-permute-start.8 = (bf16[24,768]{1,0:T(8,128)(2,1)S(1)}, bf16[24,768]{1,0:T(8,128)(2,1)S(1)}, u32[]{:S(2)}, u32[]{:S(2)}) collective-permute-start(bf16[24,768]{1,0:T(8,128)(2,1)S(1)} %fusion.68), channel_id=1, source_target_pairs={{0,16},{2,18},{4,20},{6,22},{8,24},{10,26},{12,28},{14,30},{16,0},... | collective-permute-start | bytes 110600 | tf_op jit(solution)/shard_map/ppermute | solution.py:143
  442.2 7.5 %collective-permute-start.33 = (f32[24,768]{1,0:T(8,128)S(1)}, f32[24,768]{1,0:T(8,128)S(1)}, u32[]{:S(2)}, u32[]{:S(2)}) collective-permute-start(f32[24,768]{1,0:T(8,128)S(1)} %fusion.63), channel_id=1, source_target_pairs={{0,1},{1,0},{2,3},{3,2},{4,5},{5,4},{6,7},{7,6},{8,9},{9,8},{10,11... | collective-permute-start | bytes 221192 | tf_op jit(solution)/shard_map/ppermute | solution.py:147
  442.7 28.4 %collective-permute-start.35 = (bf16[2,2,2,24,3072]{4,3,2,1,0:T(8,128)(2,1)S(1)}, bf16[2,2,2,24,3072]{4,3,2,1,0:T(8,128)(2,1)S(1)}, u32[]{:S(2)}, u32[]{:S(2)}) collective-permute-start(bf16[2,2,2,24,3072]{4,3,2,1,0:T(8,128)(2,1)S(1)} %copy.156), channel_id=1, source_target_pairs={{0,4},{2,6},{4,0},{6,2},{8,12},{10,14},{12,8},{14,10},{16,20},{18,... | collective-permute-start | bytes 3538952 | tf_op jit(solution)/shard_map/ppermute | solution.py:143
  444.9 4.9 collective-permute-start.27
  446.0 27.4 %collective-permute-start.21 = (f32[24,768]{1,0:T(8,128)S(1)}, f32[24,768]{1,0:T(8,128)S(1)}, u32[]{:S(2)}, u32[]{:S(2)}) collective-permute-start(f32[24,768]{1,0:T(8,128)S(1)} %fusion.67), channel_id=1, source_target_pairs={{0,1},{1,0},{2,3},{3,2},{4,5},{5,4},{6,7},{7,6},{8,9},{9,8},{10,11... | collective-permute-start | bytes 221192 | tf_op jit(solution)/shard_map/ppermute | solution.py:147
  446.8 28.3 %collective-permute-start.41 = (bf16[2,2,2,96,768]{4,3,2,1,0:T(8,128)(2,1)S(1)}, bf16[2,2,2,96,768]{4,3,2,1,0:T(8,128)(2,1)S(1)}, u32[]{:S(2)}, u32[]{:S(2)}) collective-permute-start(bf16[2,2,2,96,768]{4,3,2,1,0:T(8,128)(2,1)S(1)} %copy.163), channel_id=1, source_target_pairs={{0,2},{2,0},{4,6},{6,4},{8,10},{10,8},{12,14},{14,12},{16,18},{18,... | collective-permute-start | bytes 3538952 | tf_op jit(solution)/shard_map/ppermute | solution.py:143
  449.7 38.7 %collective-permute-start.9 = (f32[24,768]{1,0:T(8,128)S(1)}, f32[24,768]{1,0:T(8,128)S(1)}, u32[]{:S(2)}, u32[]{:S(2)}) collective-permute-start(f32[24,768]{1,0:T(8,128)S(1)} %fusion.69), channel_id=1, source_target_pairs={{0,1},{1,0},{2,3},{3,2},{4,5},{5,4},{6,7},{7,6},{8,9},{9,8},{10,11... | collective-permute-start | bytes 221192 | tf_op jit(solution)/shard_map/ppermute | solution.py:147
  471.3 14.9 %collective-permute-start.36 = (bf16[2,2,24,3072]{3,2,1,0:T(8,128)(2,1)S(1)}, bf16[2,2,24,3072]{3,2,1,0:T(8,128)(2,1)S(1)}, u32[]{:S(2)}, u32[]{:S(2)}) collective-permute-start(bf16[2,2,24,3072]{3,2,1,0:T(8,128)(2,1)S(1)} %copy.159), channel_id=1, source_target_pairs={{0,8},{2,10},{4,12},{6,14},{8,0},{10,2},{12,4},{14,6},{16,24},{18,... | collective-permute-start | bytes 1769480 | tf_op jit(solution)/shard_map/ppermute | solution.py:143
  475.3 14.8 %collective-permute-start.42 = (bf16[2,2,96,768]{3,2,1,0:T(8,128)(2,1)S(1)}, bf16[2,2,96,768]{3,2,1,0:T(8,128)(2,1)S(1)}, u32[]{:S(2)}, u32[]{:S(2)}) collective-permute-start(bf16[2,2,96,768]{3,2,1,0:T(8,128)(2,1)S(1)} %copy.166), channel_id=1, source_target_pairs={{0,4},{2,6},{4,0},{6,2},{8,12},{10,14},{12,8},{14,10},{16,20},{18,... | collective-permute-start | bytes 1769480 | tf_op jit(solution)/shard_map/ppermute | solution.py:143
  486.4 8.0 %collective-permute-start.37 = (bf16[2,24,3072]{2,1,0:T(8,128)(2,1)S(1)}, bf16[2,24,3072]{2,1,0:T(8,128)(2,1)S(1)}, u32[]{:S(2)}, u32[]{:S(2)}) collective-permute-start(bf16[2,24,3072]{2,1,0:T(8,128)(2,1)S(1)} %fusion.43), channel_id=1, source_target_pairs={{0,2},{2,0},{4,6},{6,4},{8,10},{10,8},{12,14},{14,12},{16,18},{18,... | collective-permute-start | bytes 884744 | tf_op jit(solution)/shard_map/ppermute | solution.py:143
  490.3 9.7 %collective-permute-start.43 = (bf16[2,96,768]{2,1,0:T(8,128)(2,1)S(1)}, bf16[2,96,768]{2,1,0:T(8,128)(2,1)S(1)}, u32[]{:S(2)}, u32[]{:S(2)}) collective-permute-start(bf16[2,96,768]{2,1,0:T(8,128)(2,1)S(1)} %fusion.42), channel_id=1, source_target_pairs={{0,8},{2,10},{4,12},{6,14},{8,0},{10,2},{12,4},{14,6},{16,24},{18,... | collective-permute-start | bytes 884744 | tf_op jit(solution)/shard_map/ppermute | solution.py:143
  494.5 13.1 %collective-permute-start.38 = (bf16[24,3072]{1,0:T(8,128)(2,1)S(1)}, bf16[24,3072]{1,0:T(8,128)(2,1)S(1)}, u32[]{:S(2)}, u32[]{:S(2)}) collective-permute-start(bf16[24,3072]{1,0:T(8,128)(2,1)S(1)} %fusion.52), channel_id=1, source_target_pairs={{0,16},{2,18},{4,20},{6,22},{8,24},{10,26},{12,28},{14,30},{16,0},... | collective-permute-start | bytes 442376 | tf_op jit(solution)/shard_map/ppermute | solution.py:143
  500.0 9.3 %collective-permute-start.44 = (bf16[96,768]{1,0:T(8,128)(2,1)S(1)}, bf16[96,768]{1,0:T(8,128)(2,1)S(1)}, u32[]{:S(2)}, u32[]{:S(2)}) collective-permute-start(bf16[96,768]{1,0:T(8,128)(2,1)S(1)} %fusion.50), channel_id=1, source_target_pairs={{0,16},{2,18},{4,20},{6,22},{8,24},{10,26},{12,28},{14,30},{16,0},... | collective-permute-start | bytes 442376 | tf_op jit(solution)/shard_map/ppermute | solution.py:143
  507.7 1.8 collective-permute-start.39
  509.5 1.6 collective-permute-start.45
  (81 other events, 1055.2 us)

commit v2 on v1

--- a/solution.py
+++ b/solution.py
@@ -1,10 +1,16 @@
 import jax
 import jax.numpy as jnp
 from jax import lax
+from jax.experimental import pallas as pl
+from jax.experimental.pallas import tpu as pltpu
 from jax.sharding import PartitionSpec as P
 
 HEAD_DIM = 64
 DOCS = 8
+MOST = 256
+BLOCK = 128
+WINDOW = 1 + 2 * MOST // BLOCK
+LOWEST = -1e30
 SWAP = [(0, 1), (1, 0)]
 
 
@@ -14,104 +20,259 @@
     return centre * lax.rsqrt(spread + 1e-12) * gain + shift
 
 
-def gelu_exact(inner):
-    return jax.nn.gelu(inner, approximate=False)
+def gelu_and_slope(inner):
+    below = 0.5 + 0.5 * lax.erf(inner * 0.5**0.5)
+    density = jnp.exp(-0.5 * inner * inner) * 0.3989422804014327
+    return inner * below, below + inner * density
 
 
 def dense(left, right):
     return jnp.dot(left, right, preferred_element_type=jnp.float32)
 
 
-def block_scores(query_block, heads_key, segment_block, segment_row):
-    valid_keys = segment_row != DOCS - 1
-    valid_block = segment_block != DOCS - 1
-    allowed = (
-        (segment_block[:, None] == segment_row[None, :])
-        & valid_block[:, None]
-        & valid_keys[None, :]
-    )
-    scores = (
-        jnp.einsum("qhd,khd->hqk", query_block, heads_key, preferred_element_type=jnp.float32)
-        * 0.125
-    )
-    return (scores, allowed[None], valid_block)
-
-
-def attend_forward(item):
-    query, key, value, segment_row = item
-    length, local = query.shape
-    heads = local // HEAD_DIM
-    block = min(512, length)
-    heads_query = query.reshape(length, heads, HEAD_DIM)
-    heads_key = key.reshape(length, heads, HEAD_DIM)
-    heads_value = value.reshape(length, heads, HEAD_DIM)
-    pieces = []
-    sums = []
-    for start in range(0, length, block):
-        scores, allowed, valid_block = block_scores(
-            heads_query[start : start + block],
-            heads_key,
-            segment_row[start : start + block],
-            segment_row,
-        )
-        largest = jnp.max(jnp.where(allowed, scores, -jnp.inf), axis=-1)
-        safe_max = jnp.where(valid_block[None, :], largest, 0.0)
-        weights = jnp.exp(jnp.where(allowed, scores - safe_max[..., None], -jnp.inf))
-        total = jnp.sum(weights, axis=-1)
-        safe_total = jnp.where(valid_block[None, :], total, 1.0)
-        probs = (weights / safe_total[..., None]).astype(jnp.bfloat16)
-        context = jnp.einsum("hqk,khd->qhd", probs, heads_value, preferred_element_type=jnp.float32)
-        pieces.append(context.reshape(block, local).astype(jnp.bfloat16))
-        sums.append(safe_max + jnp.log(safe_total))
-    return (jnp.concatenate(pieces, axis=0), jnp.concatenate(sums, axis=1))
-
-
-def attend_backward(item):
-    query, key, value, segment_row, grad_context, logsum = item
-    length, local = query.shape
-    heads = local // HEAD_DIM
-    block = min(512, length)
-    heads_query = query.reshape(length, heads, HEAD_DIM)
-    heads_key = key.reshape(length, heads, HEAD_DIM)
-    heads_value = value.reshape(length, heads, HEAD_DIM)
-    grad_key = jnp.zeros((length, heads, HEAD_DIM), jnp.float32)
-    grad_value = jnp.zeros((length, heads, HEAD_DIM), jnp.float32)
-    query_pieces = []
-    for start in range(0, length, block):
-        query_block = heads_query[start : start + block]
-        scores, allowed, valid_block = block_scores(
-            query_block, heads_key, segment_row[start : start + block], segment_row
-        )
-        probs = jnp.exp(
-            jnp.where(allowed, scores - logsum[:, start : start + block][..., None], -jnp.inf)
-        )
-        probs_low = probs.astype(jnp.bfloat16)
-        grad_block = grad_context[start : start + block].reshape(block, heads, HEAD_DIM)
-        grad_probs = jnp.einsum(
-            "qhd,khd->hqk", grad_block, heads_value, preferred_element_type=jnp.float32
-        )
-        grad_value = grad_value + jnp.einsum(
-            "hqk,qhd->khd", probs_low, grad_block, preferred_element_type=jnp.float32
-        )
-        inner = jnp.sum(grad_probs * probs, axis=-1, keepdims=True)
-        grad_scores = (probs * (grad_probs - inner)).astype(jnp.bfloat16)
-        query_grad = (
-            jnp.einsum("hqk,khd->qhd", grad_scores, heads_key, preferred_element_type=jnp.float32)
-            * 0.125
-        )
-        query_pieces.append(query_grad.reshape(block, local).astype(jnp.bfloat16))
-        grad_key = (
-            grad_key
-            + jnp.einsum(
-                "hqk,qhd->khd", grad_scores, query_block, preferred_element_type=jnp.float32
-            )
-            * 0.125
-        )
-    return (
-        jnp.concatenate(query_pieces, axis=0),
-        grad_key.reshape(length, local).astype(jnp.bfloat16),
-        grad_value.reshape(length, local).astype(jnp.bfloat16),
-    )
+def key_windows(segments):
+    length = segments.shape[0]
+    blocks = segments.reshape(length // BLOCK, BLOCK)
+    first = blocks[:, :1]
+    last = jnp.minimum(blocks[:, -1:], DOCS - 2)
+    before = jnp.sum((segments[None, :] < first).astype(jnp.int32), axis=1)
+    upto = jnp.sum((segments[None, :] <= last).astype(jnp.int32), axis=1)
+    low = before // BLOCK
+    count = jnp.clip((upto + BLOCK - 1) // BLOCK - low, 0, WINDOW)
+    count = jnp.where(first[:, 0] == DOCS - 1, 0, count)
+    return jnp.minimum(low, length // BLOCK - count), count
+
+
+def two_heads(pair):
+    lane = lax.broadcasted_iota(jnp.int32, pair.shape, 1)
+    zero = jnp.zeros_like(pair)
+    return jnp.concatenate(
+        [jnp.where(lane < HEAD_DIM, pair, zero), jnp.where(lane < HEAD_DIM, zero, pair)], axis=0
+    )
+
+
+def outer_dot(left, right):
+    return lax.dot_general(
+        left, right, (((1,), (1,)), ((), ())), preferred_element_type=jnp.float32
+    )
+
+
+def own_heads(both):
+    return jnp.concatenate([both[:HEAD_DIM, :BLOCK], both[HEAD_DIM:, BLOCK:]], axis=0)
+
+
+def pair_lanes(pair):
+    return slice(pair * BLOCK, pair * BLOCK + BLOCK)
+
+
+def forward_kernel(
+    low_ref, count_ref, seg_row, seg_col, q_ref, k_ref, v_ref, ctx_ref, log_ref, turned
+):
+    at = pl.program_id(0)
+    pairs = q_ref.shape[1] // BLOCK
+
+    @pl.when(at == 0)
+    def _():
+        turned[...] = v_ref[...].T
+
+    start = pl.multiple_of(low_ref[at] * BLOCK, BLOCK)
+    row = seg_row[0]
+    valid = row != DOCS - 1
+    row = jnp.where(valid, row, -1)
+
+    def work(count):
+        window = pl.ds(start, count * BLOCK)
+        allowed = seg_col[window, :] == row
+        all_scores = []
+        for pair in range(pairs):
+            lanes = pair_lanes(pair)
+            query = two_heads(q_ref[:, lanes] * jnp.bfloat16(0.125))
+            all_scores.append(outer_dot(k_ref[window, lanes], query))
+        logs = []
+        for pair in range(pairs):
+            lanes = pair_lanes(pair)
+            weights = []
+            inverse = []
+            for head in range(2):
+                own = jnp.where(allowed, all_scores[pair][:, pair_lanes(head)], LOWEST)
+                top = jnp.max(own, axis=0, keepdims=True)
+                exps = jnp.exp(own - top)
+                total = jnp.sum(exps, axis=0, keepdims=True)
+                weights.append(exps.astype(jnp.bfloat16))
+                inverse.append(jnp.where(valid, 1.0 / total, 0.0))
+                logs.append(jnp.where(valid, top + jnp.log(total), -LOWEST))
+            both = dense(turned[lanes, window], jnp.concatenate(weights, axis=1))
+            both = both * jnp.concatenate(inverse, axis=1)
+            ctx_ref[:, lanes] = own_heads(both).T.astype(jnp.bfloat16)
+        spare = log_ref.shape[0] - 2 * pairs
+        if spare:
+            logs.append(jnp.zeros((spare, BLOCK), jnp.float32))
+        log_ref[...] = jnp.concatenate(logs, axis=0)
+
+    @pl.when(count_ref[at] == 0)
+    def _():
+        ctx_ref[...] = jnp.zeros_like(ctx_ref)
+        log_ref[...] = jnp.full_like(log_ref, -LOWEST)
+
+    for count in range(1, WINDOW + 1):
+
+        @pl.when(count_ref[at] == count)
+        def _():
+            work(count)
+
+
+def backward_kernel(
+    low_ref,
+    count_ref,
+    seg_row,
+    seg_col,
+    q_ref,
+    k_ref,
+    v_ref,
+    g_ref,
+    log_ref,
+    dq_ref,
+    dk_ref,
+    dv_ref,
+    turned,
+    dk_sum,
+    dv_sum,
+):
+    at = pl.program_id(0)
+    pairs = q_ref.shape[1] // BLOCK
+
+    @pl.when(at == 0)
+    def _():
+        turned[...] = k_ref[...].T
+        dk_sum[...] = jnp.zeros_like(dk_sum)
+        dv_sum[...] = jnp.zeros_like(dv_sum)
+
+    start = pl.multiple_of(low_ref[at] * BLOCK, BLOCK)
+    row = seg_row[0]
+    row = jnp.where(row != DOCS - 1, row, -1)
+
+    def work(count):
+        window = pl.ds(start, count * BLOCK)
+        allowed = seg_col[window, :] == row
+
+        def products(pair):
+            lanes = pair_lanes(pair)
+            query = two_heads(q_ref[:, lanes] * jnp.bfloat16(0.125))
+            grad = two_heads(g_ref[:, lanes])
+            scores = outer_dot(k_ref[window, lanes], query)
+            return query, grad, scores, outer_dot(v_ref[window, lanes], grad)
+
+        def softmax(pair, query, grad, scores, grad_probs):
+            probs_low = []
+            grad_scores = []
+            for head in range(2):
+                cols = pair_lanes(head)
+                log = log_ref[2 * pair + head : 2 * pair + head + 1, :]
+                probs = jnp.exp(jnp.where(allowed, scores[:, cols], LOWEST) - log)
+                own = grad_probs[:, cols]
+                inner = jnp.sum(probs * own, axis=0, keepdims=True)
+                probs_low.append(probs.astype(jnp.bfloat16))
+                grad_scores.append((probs * (own - inner)).astype(jnp.bfloat16))
+            joined = [jnp.concatenate(p, axis=1) for p in (probs_low, grad_scores)]
+            return query, grad, *joined
+
+        def results(pair, query, grad, probs_low, grad_scores):
+            lanes = pair_lanes(pair)
+            dv_sum[window, lanes] += dense(probs_low, grad)
+            dk_sum[window, lanes] += dense(grad_scores, query)
+            both = dense(turned[lanes, window], grad_scores)
+            dq_ref[:, lanes] = (own_heads(both).T * 0.125).astype(jnp.bfloat16)
+
+        ahead = products(0)
+        behind = None
+        for pair in range(pairs):
+            now = ahead
+            if pair + 1 < pairs:
+                ahead = products(pair + 1)
+            done = softmax(pair, *now)
+            if pair > 0:
+                results(pair - 1, *behind)
+            behind = done
+        results(pairs - 1, *behind)
+
+    @pl.when(count_ref[at] == 0)
+    def _():
+        dq_ref[...] = jnp.zeros_like(dq_ref)
+
+    for count in range(1, WINDOW + 1):
+
+        @pl.when(count_ref[at] == count)
+        def _():
+            work(count)
+
+    @pl.when(at == pl.num_programs(0) - 1)
+    def _():
+        dk_ref[...] = dk_sum[...].astype(jnp.bfloat16)
+        dv_ref[...] = dv_sum[...].astype(jnp.bfloat16)
+
+
+def attention_call(kernel, name, arrays, outputs, scratch, shape, flops):
+    length, width = shape
+    log_rows = width // HEAD_DIM + -(width // HEAD_DIM) % 8
+    kinds = {
+        "row": (pl.BlockSpec((1, 1, BLOCK), lambda i, *_: (i, 0, 0)), None),
+        "col": (pl.BlockSpec((length, BLOCK), lambda i, *_: (0, 0)), None),
+        "block": (
+            pl.BlockSpec((BLOCK, width), lambda i, *_: (i, 0)),
+            jax.ShapeDtypeStruct((length, width), jnp.bfloat16),
+        ),
+        "whole": (
+            pl.BlockSpec((length, width), lambda i, *_: (0, 0)),
+            jax.ShapeDtypeStruct((length, width), jnp.bfloat16),
+        ),
+        "logs": (
+            pl.BlockSpec((log_rows, BLOCK), lambda i, *_: (0, i)),
+            jax.ShapeDtypeStruct((log_rows, length), jnp.float32),
+        ),
+    }
+    return pl.pallas_call(
+        kernel,
+        grid_spec=pltpu.PrefetchScalarGridSpec(
+            num_scalar_prefetch=2,
+            grid=(length // BLOCK,),
+            in_specs=[kinds[k][0] for k in arrays],
+            out_specs=[kinds[k][0] for k in outputs],
+            scratch_shapes=scratch,
+        ),
+        out_shape=[kinds[k][1] for k in outputs],
+        cost_estimate=pl.CostEstimate(
+            flops=flops, bytes_accessed=2 * length * width * len(arrays), transcendentals=0
+        ),
+        name=name,
+    )
+
+
+def attend_forward(query, key, value, segments):
+    length, width = query.shape
+    call = attention_call(
+        forward_kernel,
+        "attend_forward",
+        ["row", "col", "block", "whole", "whole"],
+        ["block", "logs"],
+        [pltpu.VMEM((width, length), jnp.bfloat16)],
+        (length, width),
+        16 * length * width * BLOCK * WINDOW,
+    )
+    return call(*segments, query, key, value)
+
+
+def attend_backward(query, key, value, segments, grad_context, logs):
+    length, width = query.shape
+    call = attention_call(
+        backward_kernel,
+        "attend_backward",
+        ["row", "col", "block", "whole", "whole", "block", "logs"],
+        ["block", "whole", "whole"],
+        [pltpu.VMEM((width, length), jnp.bfloat16)] + [pltpu.VMEM((length, width), jnp.float32)] * 2,
+        (length, width),
+        32 * length * width * BLOCK * WINDOW,
+    )
+    return call(*segments, query, key, value, grad_context, logs)
 
 
 def pick(array, index, axis):
@@ -195,7 +356,15 @@
     query = (dense(flattened, query_weight) + query_bias.astype(jnp.float32)).astype(jnp.bfloat16)
     key = dense(flattened, key_weight).astype(jnp.bfloat16)
     value = (dense(flattened, value_weight) + value_bias.astype(jnp.float32)).astype(jnp.bfloat16)
-    context_rows, logsum = attend_forward((query, key, value, segment_row))
+    length = 2 * half
+    low, count = key_windows(segment_row)
+    place = (
+        low,
+        count,
+        segment_row.reshape(length // BLOCK, 1, BLOCK),
+        jnp.broadcast_to(segment_row[:, None], (length, BLOCK)),
+    )
+    context_rows, logsum = attend_forward(query, key, value, place)
     attended = dense(context_rows, output_weight) + output_bias.astype(jnp.float32)
     first_sum = flattened.astype(jnp.float32) + attended
     first_norm, first_back = jax.vjp(
@@ -203,8 +372,9 @@
     )
     norm_low = first_norm.astype(jnp.bfloat16)
     inner = dense(norm_low, inner_weight) + inner_bias.astype(jnp.float32)
-    activation, gelu_back = jax.vjp(gelu_exact, inner)
+    activation, slope = gelu_and_slope(inner)
     act_low = activation.astype(jnp.bfloat16)
+    slope = slope.astype(jnp.bfloat16)
     outer = dense(act_low, outer_weight) + outer_bias.astype(jnp.float32)
     second_sum = first_norm + outer
     result, second_back = jax.vjp(
@@ -216,8 +386,8 @@
     outer_weight_term = dense(act_low.T, grad_outer)
     outer_weight_grad = scatter_sum(outer_weight_term, (0, 1, 2, 3))
     outer_bias_term = jnp.sum(grad_outer.astype(jnp.float32), axis=0)
-    (grad_inner_full,) = gelu_back(dense(grad_outer, outer_weight.T))
-    grad_inner = grad_inner_full.astype(jnp.bfloat16)
+    grad_inner = dense(grad_outer, outer_weight.T) * slope.astype(jnp.float32)
+    grad_inner = grad_inner.astype(jnp.bfloat16)
     inner_weight_term = dense(norm_low.T, grad_inner)
     inner_weight_grad = scatter_sum(inner_weight_term, (1, 2, 0, 3))
     inner_bias_term = jnp.sum(grad_inner.astype(jnp.float32), axis=0)
@@ -228,7 +398,7 @@
     output_bias_term = jnp.sum(grad_attn.astype(jnp.float32), axis=0)
     grad_context = dense(grad_attn, output_weight.T).astype(jnp.bfloat16)
     grad_query, grad_key, grad_value = attend_backward(
-        (query, key, value, segment_row, grad_context, logsum)
+        query, key, value, place, grad_context, logsum
     )
     query_weight_term = dense(flattened.T, grad_query)
     query_bias_term = jnp.sum(grad_query.astype(jnp.float32), axis=0)

time: 523 us -> 316 us (0.60); the launches traced: 512 us -> 312 us
  matrix products: 254 us -> 92 us
  other arithmetic: 118 us -> 50.9 us
  Pallas kernels: 0 us -> 38.2 us
  local copies, waits for them, and re-layouts: 35.7 us -> 27.3 us
  starting transfers between devices: 46.2 us -> 38.5 us
  waiting for transfers between devices: 55.9 us -> 62.9 us
    dot_general x12 -> x0, matrix products: 140 us -> none  [the longest x2 36.1 us: attend_backward(): jnp.einsum('qhd,khd->hqk', grad_block, heads_value, preferred_element_typ...]
    convert_element_type x2 -> x0, other arithmetic: 43.4 us -> none  [attend_backward(): grad_scores = (probs * (grad_probs - inner)).astype(jnp.bfloat16)]
    pallas_call x0 -> x2, Pallas kernels: none -> 38.2 us  [the longest x1 22.8 us: attend_backward(): return call(*segments, query, key, value, grad_context, logs)]
    reduce_sum x3 -> x2, other arithmetic: 24.7 us -> 0.71 us  [the longest x1 0.49 us: shards(): value_bias_term = jnp.sum(grad_value.astype(jnp.float32), axis=0)]
    dot_general x18, matrix products: 114 us -> 92 us  [dense(): return jnp.dot(left, right, preferred_element_type=jnp.float32)]
    unnamed x167 -> x143, local copies, waits for them, and re-layouts: 10.3 us -> 1.57 us
    ppermute x28, starting transfers between devices: 42.3 us -> 34.6 us  [scatter_sum(): got = lax.ppermute(sent, 'dp', [(i, i ^ 1 << bit) for i in range(size)])]
    ppermute x28, waiting for transfers between devices: 55.2 us -> 62.2 us  [scatter_sum(): got = lax.ppermute(sent, 'dp', [(i, i ^ 1 << bit) for i in range(size)])]
  transfers between devices with their start and end apart: 46 -> 46, of which waited for: 14 -> 13; matrix products, arithmetic and copies ran while one was open for 40% -> 30% of each run, Pallas kernels for 0% -> 5%
where the time goes in v2:
time: 316 us; the launch traced here: 312 us
  matrix products  92 us (29%)
  waiting for transfers between devices  62.9 us (20%)
  other arithmetic  50.9 us (16%)
  starting transfers between devices  38.5 us (12%)
  Pallas kernels  38.2 us (12%)
  local copies, waits for them, and re-layouts  27.3 us (9%)
    dot_general x18, matrix products, dense(): return jnp.dot(left, right, preferred_element_type=jnp.float32)  92 us
    ppermute x28, waiting for transfers between devices, scatter_sum(): got = lax.ppermute(sent, 'dp', [(i, i ^ 1 << bit) for i in range(size)])  62.2 us
    ppermute x28, starting transfers between devices, scatter_sum(): got = lax.ppermute(sent, 'dp', [(i, i ^ 1 << bit) for i in range(size)])  34.6 us
    pallas_call x1, Pallas kernels, attend_backward(): return call(*segments, query, key, value, grad_context, logs)  22.8 us
    convert_element_type x28, other arithmetic, scatter_sum(): total_of([pick(part, 1 - mine, axis) for part in parts])  16 us
    convert_element_type x7, local copies, waits for them, and re-layouts, scatter_sum(): sent = pick(term, 1 - core, bits).astype(jnp.bfloat16)  15.8 us
    pallas_call x1, Pallas kernels, attend_forward(): return call(*segments, query, key, value)  15.3 us
  transfers between devices with their start and end apart: 46, of which 13 were waited for; matrix products, arithmetic and copies ran while one was open for 30% of the time, Pallas kernels for 5%

profile of v2, /device:TPU:0, one launch (start us, length us, event | category | flops | bytes accessed | tf_op | source)
XLA Modules:
  0.0 312.3 jit_solution(13638542518741342370)
XLA Ops:
  0.7 2.2 dynamic-slice_bitcast_fusion.3
  17.3 2.5 convolution_convert_fusion.1.k_ref
  19.9 2.6 add_convert_fusion.3.q_ref
  22.5 2.6 add_convert_fusion.2.v_ref
  26.1 15.3 %attend_forward.1 = (bf16[1024,768]{1,0:T(8,128)(2,1)}, f32[16,1024]{1,0:T(8,128)}) custom-call(s32[8]{0:T(128)} %get-tuple-element.45.low_ref, s32[8]{0:T(128)} %get-tuple-element.46.count_ref, s32[8,1,128]{2,1,0:T(1,128)} %fusion.172.seg_row, s32[1024,128]{1,0:T(8,128)} %broadcast_in_dim.12.seg_col, bf16[1024,768]{1,0:T(8,128)(2,1)} %add_convert_fusion.3.q_ref, ...), custom_call_target="tpu_custom_call" | custom-call | flops 8053063680 | bytes 7864320 | tf_op jit(solution)/shard_map/attend_forward/pallas_call | solution.py:261
  41.4 3.1 fusion.138
  45.3 9.6 %multiply_convert_fusion.1 = (bf16[1024,3072]{1,0:T(8,128)(2,1)S(1)}, f32[1024,3072]{1,0:T(8,128)}) fusion(f32[3072]{0:T(1024)S(1)} %copy-done.41, bf16[768,3072]{1,0:T(8,128)(2,1)S(1)} %bitcast.696, f32[1024,768]{1,0:T(8,128)S(1)} %get-tuple-element.79, f32[768]{0:T(1024)S(1)} %convert_element_type.992, f32[768]{0:T(1024)S(1)} %convert_element_type.991, ...), kind=kOutput, calls=%fused_computation.8 | convolution fusion | flops 4854644736 | bytes 26765312 | tf_op jit(solution)/shard_map/dot_general | solution.py:30
  54.9 5.5 %fusion.139 = (f32[1024]{0:T(1024)S(1)}, f32[1024,768]{1,0:T(8,128)S(1)}) fusion(f32[768]{0:T(1024)S(1)} %copy-done.45, bf16[1024,3072]{1,0:T(8,128)(2,1)S(1)} %get-tuple-element.80, bf16[3072,768]{1,0:T(8,128)(2,1)S(1)} %bitcast.694, f32[768]{0:T(1024)S(1)} %convert_element_type.992, f32[768]{0:T(1024)S(1)} %convert_element_type.991, ...), kind=kOutput, calls=%fused_computation.404 | convolution fusion | flops 4837342208 | bytes 17323008 | tf_op jit(solution)/shard_map/dot_general | solution.py:30
  63.1 3.0 fusion.8
  66.0 2.4 fusion.136
  69.6 13.3 %convert_reduce_fusion = (f32[3072]{0:T(1024)}, bf16[1024,3072]{1,0:T(8,128)(2,1)S(1)}) fusion(f32[1024,3072]{1,0:T(8,128)} %get-tuple-element.81, f32[3072]{0:T(1024)S(1)} %copy-done.41, bf16[1024,768]{1,0:T(8,128)(2,1)S(1)} %get-tuple-element.38, bf16[3072,768]{1,0:T(8,128)(2,1)S(1)} %bitcast.694), kind=kOutput, calls=%fused_computation.6 | convolution fusion | flops 4879021056 | bytes 25190400 | tf_op jit(solution)/shard_map/dot_general | solution.py:30
  82.9 11.3 %multiply_reduce_fusion = (f32[768]{0:T(1024)}, f32[1024]{0:T(1024)S(1)}, f32[768]{0:T(1024)}, f32[1024,768]{1,0:T(8,128)S(1)}) fusion(f32[1024,768]{1,0:T(8,128)S(1)} %get-tuple-element.79, f32[1024]{0:T(1024)S(1)} %fusion.86, f32[1024]{0:T(1024)S(1)} %broadcast_multiply_fusion.1, f32[768]{0:T(1024)S(1)} %convert_element_type.991, ...), kind=kOutput, calls=%fused_computation.22 | convolution fusion | flops 4839699456 | bytes 20472832 | tf_op jit(solution)/shard_map/dot_general | solution.py:30
  97.0 2.6 convolution_convert_fusion.g_ref
  99.5 22.8 %attend_backward.1 = (bf16[1024,768]{1,0:T(8,128)(2,1)}, bf16[1024,768]{1,0:T(8,128)(2,1)}, bf16[1024,768]{1,0:T(8,128)(2,1)}) custom-call(s32[8]{0:T(128)} %get-tuple-element.45.low_ref, s32[8]{0:T(128)} %get-tuple-element.46.count_ref, s32[8,1,128]{2,1,0:T(1,128)} %fusion.172.seg_row, s32[1024,128]{1,0:T(8,128)} %broadcast_in_dim.12.seg_col, ...), custom_call_target="tpu_custom_call" | custom-call | flops 16106127360 | bytes 11010048 | tf_op jit(solution)/shard_map/attend_backward/pallas_call | solution.py:275
  122.4 5.0 %fusion.140 = f32[1024,768]{1,0:T(8,128)} fusion(bf16[1024,768]{1,0:T(8,128)(2,1)} %get-tuple-element.24, bf16[768,768]{1,0:T(8,128)(2,1)} %param.20), kind=kOutput, calls=%fused_computation.405 | convolution fusion | flops 1207959552 | bytes 5898240 | tf_op jit(solution)/shard_map/dot_general | solution.py:30
  129.1 3.1 fusion.141
  132.2 2.9 fusion.133
  135.6 2.9 fusion.132
  138.5 2.8 fusion.142
  141.4 8.4 %fusion.128 = f32[768,3072]{1,0:T(8,128)} fusion(bf16[1024,3072]{1,0:T(8,128)(2,1)S(1)} %bitcast.652, f32[1024,768]{1,0:T(8,128)S(1)} %copy-done.3, f32[768]{0:T(1024)S(1)} %convert_element_type.992, f32[768]{0:T(1024)S(1)} %convert_element_type.991, f32[1024]{0:T(1024)S(1)} %fusion.86, f32[1024]{0:T(1024)S(1)} %broadcast_multiply_fusion.1), kind=kOutput, calls=%fused_computation.395 | convolution fusion | flops 4835770368 | bytes 18888704 | tf_op jit(solution)/shard_map/dot_general | solution.py:30
  149.9 8.0 %fusion.143 = f32[3072,768]{1,0:T(8,128)} fusion(bf16[1024,3072]{1,0:T(8,128)(2,1)S(1)} %bitcast.698, bf16[1024,768]{1,0:T(8,128)(2,1)S(1)} %copy-done.16), kind=kOutput, calls=%fused_computation.408 | convolution fusion | flops 4831838208 | bytes 17301504 | tf_op jit(solution)/shard_map/dot_general | solution.py:30
  160.4 2.1 fusion.21
  163.1 2.4 fusion.22
  165.6 4.1 %fusion.10 = bf16[2,2,2,2,24,3072]{5,4,0,3,2,1:T(8,128)(2,1)} fusion(f32[2,2,2,2,2,24,3072]{6,5,4,3,2,1,0:T(8,128)} %bitcast.643, s32[]{:T(128)S(6)} %select_n.423), kind=kLoop, calls=%fused_computation.40 | loop fusion | bytes 4718596 | tf_op jit(solution)/shard_map/convert_element_type | solution.py:297
  170.0 3.5 %collective-permute-done.11 = bf16[2,2,2,1,384]{4,1,0,3,2:T(2,128)(2,1)S(1)} collective-permute-done((bf16[2,2,2,1,384]{4,1,0,3,2:T(2,128)(2,1)S(1)}, bf16[2,2,2,1,384]{4,1,0,3,2:T(2,128)(2,1)S(1)}, u32[]{:S(2)}, u32[]{:S(2)}) %collective-permute-start.11) | collective-permute-done | bytes 6176 | tf_op jit(solution)/shard_map/ppermute | solution.py:304
  173.5 4.9 %collective-permute-start.12 = (bf16[2,2,1,384]{3,1,2,0:T(2,128)(2,1)S(1)}, bf16[2,2,1,384]{3,1,2,0:T(2,128)(2,1)S(1)}, u32[]{:S(2)}, u32[]{:S(2)}) collective-permute-start(bf16[2,2,1,384]{3,1,2,0:T(2,128)(2,1)S(1)} %fusion.85), channel_id=1, source_target_pairs={{0,2},{2,0},{4,6},{6,4},{8,10},{10,8},{12,14},{14,12},{16,18},{18,... | collective-permute-start | bytes 9224 | tf_op jit(solution)/shard_map/ppermute | solution.py:304
  178.3 4.5 %add_convert_fusion = bf16[1024,768]{1,0:T(8,128)(2,1)S(1)} fusion(f32[1024,768]{1,0:T(8,128)} %fusion.141, f32[1024,768]{1,0:T(8,128)} %fusion.140, f32[1024,768]{1,0:T(8,128)S(1)} %copy-done.5, bf16[1024,768]{1,0:T(8,128)(2,1)S(1)} %copy-done.8, bf16[768,768]{1,0:T(8,128)(2,1)S(1)} %copy-done.22, f32[1024]{0:T(1024)S(1)} %copy-done.33), kind=kOutput, calls=%fused_computation.26 | convolution fusion | flops 1211891712 | bytes 13766656 | tf_op jit(solution)/shard_map/dot_general | solution.py:30
  183.7 4.0 %fusion.11 = bf16[2,2,2,2,96,768]{5,4,0,3,2,1:T(8,128)(2,1)} fusion(f32[2,2,2,2,2,96,768]{6,5,4,3,2,1,0:T(8,128)} %bitcast.657, s32[]{:T(128)S(6)} %select_n.423), kind=kLoop, calls=%fused_computation.41 | loop fusion | bytes 4718596 | tf_op jit(solution)/shard_map/convert_element_type | solution.py:297
  188.5 2.3 collective-permute-start.14
  193.8 2.2 fusion.23
  202.4 2.1 collective-permute-start.17
  206.5 1.7 collective-permute-start.29
  212.1 1.6 collective-permute-start.6
  215.2 5.7 %collective-permute-done.29 = bf16[2,2,2,24,768]{4,3,2,1,0:T(8,128)(2,1)S(1)} collective-permute-done((bf16[2,2,2,24,768]{4,3,2,1,0:T(8,128)(2,1)S(1)}, bf16[2,2,2,24,768]{4,3,2,1,0:T(8,128)(2,1)S(1)}, u32[]{:S(2)}, u32[]{:S(2)}) %collective-permute-start.29) | collective-permute-done | bytes 294944 | tf_op jit(solution)/shard_map/ppermute | solution.py:304
  222.0 2.1 collective-permute-start.24
  226.7 1.8 collective-permute-done.24
  228.4 1.6 collective-permute-start.19
  231.7 1.5 collective-permute-start.31
  236.0 2.2 collective-permute-start.20
  240.0 2.2 collective-permute-start.32
  248.2 23.8 %collective-permute-done.35 = bf16[2,2,2,24,3072]{4,3,2,1,0:T(8,128)(2,1)S(1)} collective-permute-done((bf16[2,2,2,24,3072]{4,3,2,1,0:T(8,128)(2,1)S(1)}, bf16[2,2,2,24,3072]{4,3,2,1,0:T(8,128)(2,1)S(1)}, u32[]{:S(2)}, u32[]{:S(2)}) %collective-permute-start.35) | collective-permute-done | bytes 1179680 | tf_op jit(solution)/shard_map/ppermute | solution.py:304
  273.4 1.8 collective-permute-done.41
  277.7 9.4 %collective-permute-done.36 = bf16[2,2,24,3072]{3,2,1,0:T(8,128)(2,1)S(1)} collective-permute-done((bf16[2,2,24,3072]{3,2,1,0:T(8,128)(2,1)S(1)}, bf16[2,2,24,3072]{3,2,1,0:T(8,128)(2,1)S(1)}, u32[]{:S(2)}, u32[]{:S(2)}) %collective-permute-start.36) | collective-permute-done | bytes 589856 | tf_op jit(solution)/shard_map/ppermute | solution.py:304
  287.9 2.2 collective-permute-done.42
  290.8 4.3 %collective-permute-done.37 = bf16[2,24,3072]{2,1,0:T(8,128)(2,1)S(1)} collective-permute-done((bf16[2,24,3072]{2,1,0:T(8,128)(2,1)S(1)}, bf16[2,24,3072]{2,1,0:T(8,128)(2,1)S(1)}, u32[]{:S(2)}, u32[]{:S(2)}) %collective-permute-start.37) | collective-permute-done | bytes 294944 | tf_op jit(solution)/shard_map/ppermute | solution.py:304
  296.7 2.2 collective-permute-done.43
  299.0 3.1 %collective-permute-start.44 = (bf16[96,768]{1,0:T(8,128)(2,1)S(1)}, bf16[96,768]{1,0:T(8,128)(2,1)S(1)}, u32[]{:S(2)}, u32[]{:S(2)}) collective-permute-start(bf16[96,768]{1,0:T(8,128)(2,1)S(1)} %fusion.30), channel_id=1, source_target_pairs={{0,16},{2,18},{4,20},{6,22},{8,24},{10,26},{12,28},{14,30},{16,0},... | collective-permute-start | bytes 442376 | tf_op jit(solution)/shard_map/ppermute | solution.py:304
  302.1 5.4 %collective-permute-done.38 = bf16[24,3072]{1,0:T(8,128)(2,1)S(1)} collective-permute-done((bf16[24,3072]{1,0:T(8,128)(2,1)S(1)}, bf16[24,3072]{1,0:T(8,128)(2,1)S(1)}, u32[]{:S(2)}, u32[]{:S(2)}) %collective-permute-start.38) | collective-permute-done | bytes 147488 | tf_op jit(solution)/shard_map/ppermute | solution.py:304
  (342 shorter events, 73.3 us)
Async XLA Ops:
  2.9 13.1 %collective-permute-start = (bf16[512,768]{1,0:T(8,128)(2,1)}, bf16[512,768]{1,0:T(8,128)(2,1)}, u32[]{:S(2)}, u32[]{:S(2)}) collective-permute-start(bf16[512,768]{1,0:T(8,128)(2,1)} %dynamic-slice_bitcast_fusion.3), channel_id=1, source_target_pairs={{0,1},{1,0},{2,3},{3,2},{4,5},{5,4},{6,7},{7,6},{8,9},{9,8},{10,11... | collective-permute-start | bytes 2359304 | tf_op jit(solution)/shard_map/ppermute | solution.py:340
  4.6 56.3 %collective-permute-start.2 = (bf16[512,768]{1,0:T(8,128)(2,1)S(1)}, bf16[512,768]{1,0:T(8,128)(2,1)}, u32[]{:S(2)}, u32[]{:S(2)}) collective-permute-start(bf16[512,768]{1,0:T(8,128)(2,1)S(1)} %dynamic-slice_bitcast_fusion.1), channel_id=1, source_target_pairs={{0,1},{1,0},{2,3},{3,2},{4,5},{5,4},{6,7},{7,6},{8,9},{9,8},{10,11... | collective-permute-start | bytes 2359304 | tf_op jit(solution)/shard_map/ppermute | solution.py:340
  44.5 49.6 %copy-start.2 = (f32[1024,768]{1,0:T(8,128)}, f32[1024,768]{1,0:T(8,128)S(1)}, u32[]{:S(2)}) copy-start(f32[1024,768]{1,0:T(8,128)S(1)} %get-tuple-element.79) | copy-start | bytes 9437188
  68.5 89.4 %copy-start.9 = (bf16[1024,768]{1,0:T(8,128)(2,1)}, bf16[1024,768]{1,0:T(8,128)(2,1)S(1)}, u32[]{:S(2)}) copy-start(bf16[1024,768]{1,0:T(8,128)(2,1)S(1)} %get-tuple-element.47) | copy-start | bytes 4718596
  158.0 46.6 %collective-permute-start.1 = (bf16[512,768]{1,0:T(8,128)(2,1)S(1)}, bf16[512,768]{1,0:T(8,128)(2,1)}, u32[]{:S(2)}, u32[]{:S(2)}) collective-permute-start(bf16[512,768]{1,0:T(8,128)(2,1)S(1)} %dynamic-slice_bitcast_fusion.2), channel_id=1, source_target_pairs={{0,1},{1,0},{2,3},{3,2},{4,5},{5,4},{6,7},{7,6},{8,9},{9,8},{10,11... | collective-permute-start | bytes 2359304 | tf_op jit(solution)/shard_map/ppermute | solution.py:348
  158.9 37.6 %collective-permute-start.4 = (bf16[2,2,2,2,24,768]{5,4,0,3,2,1:T(8,128)(2,1)}, bf16[2,2,2,2,24,768]{5,4,0,3,2,1:T(8,128)(2,1)}, u32[]{:S(2)}, u32[]{:S(2)}) collective-permute-start(bf16[2,2,2,2,24,768]{5,4,0,3,2,1:T(8,128)(2,1)} %fusion.20), channel_id=1, source_target_pairs={{0,1},{1,0},{2,3},{3,2},{4,5},{5,4},{6,7},{7,6},{8,9},{9,8},{10,11... | collective-permute-start | bytes 1769480 | tf_op jit(solution)/shard_map/ppermute | solution.py:298
  160.3 9.4 %collective-permute-start.10 = (bf16[2,2,2,2,1,384]{5,3,2,1,0,4:T(2,128)(2,1)S(1)}, bf16[2,2,2,2,1,384]{5,3,2,1,0,4:T(2,128)(2,1)S(1)}, u32[]{:S(2)}, u32[]{:S(2)}) collective-permute-start(bf16[2,2,2,2,1,384]{5,3,2,1,0,4:T(2,128)(2,1)S(1)} %bitcast.692), channel_id=1, source_target_pairs={{0,1},{1,0},{2,3},{3,2},{4,5},{5,4},{6,7},{7,6},{8,9},{9,8},{10,11... | collective-permute-start | bytes 36872 | tf_op jit(solution)/shard_map/ppermute | solution.py:298
  162.6 36.5 %collective-permute-start.16 = (bf16[2,2,2,2,24,768]{5,4,0,3,2,1:T(8,128)(2,1)}, bf16[2,2,2,2,24,768]{5,4,0,3,2,1:T(8,128)(2,1)}, u32[]{:S(2)}, u32[]{:S(2)}) collective-permute-start(bf16[2,2,2,2,24,768]{5,4,0,3,2,1:T(8,128)(2,1)} %fusion.21), channel_id=1, source_target_pairs={{0,1},{1,0},{2,3},{3,2},{4,5},{5,4},{6,7},{7,6},{8,9},{9,8},{10,11... | collective-permute-start | bytes 1769480 | tf_op jit(solution)/shard_map/ppermute | solution.py:298
  165.5 35.5 %collective-permute-start.22 = (bf16[2,2,2,2,24,768]{5,4,0,3,2,1:T(8,128)(2,1)}, bf16[2,2,2,2,24,768]{5,4,0,3,2,1:T(8,128)(2,1)}, u32[]{:S(2)}, u32[]{:S(2)}) collective-permute-start(bf16[2,2,2,2,24,768]{5,4,0,3,2,1:T(8,128)(2,1)} %fusion.22), channel_id=1, source_target_pairs={{0,1},{1,0},{2,3},{3,2},{4,5},{5,4},{6,7},{7,6},{8,9},{9,8},{10,11... | collective-permute-start | bytes 1769480 | tf_op jit(solution)/shard_map/ppermute | solution.py:298
  169.8 3.7 %collective-permute-start.11 = (bf16[2,2,2,1,384]{4,1,0,3,2:T(2,128)(2,1)S(1)}, bf16[2,2,2,1,384]{4,1,0,3,2:T(2,128)(2,1)S(1)}, u32[]{:S(2)}, u32[]{:S(2)}) collective-permute-start(bf16[2,2,2,1,384]{4,1,0,3,2:T(2,128)(2,1)S(1)} %fusion.83), channel_id=1, source_target_pairs={{0,8},{2,10},{4,12},{6,14},{8,0},{10,2},{12,4},{14,6},{16,24},{18,... | collective-permute-start | bytes 18440 | tf_op jit(solution)/shard_map/ppermute | solution.py:304
  173.5 9.4 %collective-permute-start.12 = (bf16[2,2,1,384]{3,1,2,0:T(2,128)(2,1)S(1)}, bf16[2,2,1,384]{3,1,2,0:T(2,128)(2,1)S(1)}, u32[]{:S(2)}, u32[]{:S(2)}) collective-permute-start(bf16[2,2,1,384]{3,1,2,0:T(2,128)(2,1)S(1)} %fusion.85), channel_id=1, source_target_pairs={{0,2},{2,0},{4,6},{6,4},{8,10},{10,8},{12,14},{14,12},{16,18},{18,... | collective-permute-start | bytes 9224 | tf_op jit(solution)/shard_map/ppermute | solution.py:304
  183.6 4.1 %collective-permute-start.13 = (bf16[2,1,384]{2,1,0:T(2,128)(2,1)S(1)}, bf16[2,1,384]{2,1,0:T(2,128)(2,1)S(1)}, u32[]{:S(2)}, u32[]{:S(2)}) collective-permute-start(bf16[2,1,384]{2,1,0:T(2,128)(2,1)S(1)} %fusion.99), channel_id=1, source_target_pairs={{0,4},{2,6},{4,0},{6,2},{8,12},{10,14},{12,8},{14,10},{16,20},{18,... | collective-permute-start | bytes 4616 | tf_op jit(solution)/shard_map/ppermute | solution.py:304
  188.5 4.5 %collective-permute-start.14 = (bf16[1,384]{1,0:T(2,128)(2,1)S(1)}, bf16[1,384]{1,0:T(2,128)(2,1)S(1)}, u32[]{:S(2)}, u32[]{:S(2)}) collective-permute-start(bf16[1,384]{1,0:T(2,128)(2,1)S(1)} %fusion.127), channel_id=1, source_target_pairs={{0,16},{2,18},{4,20},{6,22},{8,24},{10,26},{12,28},{14,30},{16,0},... | collective-permute-start | bytes 2312 | tf_op jit(solution)/shard_map/ppermute | solution.py:304
  193.7 2.3 collective-permute-start.15
  196.0 6.4 %collective-permute-start.28 = (bf16[2,2,2,2,24,768]{5,4,0,3,2,1:T(8,128)(2,1)}, bf16[2,2,2,2,24,768]{5,4,0,3,2,1:T(8,128)(2,1)S(1)}, u32[]{:S(2)}, u32[]{:S(2)}) collective-permute-start(bf16[2,2,2,2,24,768]{5,4,0,3,2,1:T(8,128)(2,1)} %fusion.23), channel_id=1, source_target_pairs={{0,1},{1,0},{2,3},{3,2},{4,5},{5,4},{6,7},{7,6},{8,9},{9,8},{10,11... | collective-permute-start | bytes 1769480 | tf_op jit(solution)/shard_map/ppermute | solution.py:298
  196.5 10.0 %collective-permute-start.3 = (bf16[512,768]{1,0:T(8,128)(2,1)}, bf16[512,768]{1,0:T(8,128)(2,1)S(1)}, u32[]{:S(2)}, u32[]{:S(2)}) collective-permute-start(bf16[512,768]{1,0:T(8,128)(2,1)} %dynamic-slice_bitcast_fusion), channel_id=1, source_target_pairs={{0,1},{1,0},{2,3},{3,2},{4,5},{5,4},{6,7},{7,6},{8,9},{9,8},{10,11... | collective-permute-start | bytes 2359304 | tf_op jit(solution)/shard_map/ppermute | solution.py:348
  199.1 44.0 %collective-permute-start.34 = (bf16[2,2,2,2,24,3072]{5,4,0,3,2,1:T(8,128)(2,1)}, bf16[2,2,2,2,24,3072]{5,4,0,3,2,1:T(8,128)(2,1)S(1)}, u32[]{:S(2)}, u32[]{:S(2)}) collective-permute-start(bf16[2,2,2,2,24,3072]{5,4,0,3,2,1:T(8,128)(2,1)} %fusion.10), channel_id=1, source_target_pairs={{0,1},{1,0},{2,3},{3,2},{4,5},{5,4},{6,7},{7,6},{8,9},{9,8},{10,11... | collective-permute-start | bytes 7077896 | tf_op jit(solution)/shard_map/ppermute | solution.py:298
  201.0 9.8 %collective-permute-start.5 = (bf16[2,2,2,24,768]{4,3,2,1,0:T(8,128)(2,1)S(1)}, bf16[2,2,2,24,768]{4,3,2,1,0:T(8,128)(2,1)S(1)}, u32[]{:S(2)}, u32[]{:S(2)}) collective-permute-start(bf16[2,2,2,24,768]{4,3,2,1,0:T(8,128)(2,1)S(1)} %copy.172), channel_id=1, source_target_pairs={{0,2},{2,0},{4,6},{6,4},{8,10},{10,8},{12,14},{14,12},{16,18},{18,... | collective-permute-start | bytes 884744 | tf_op jit(solution)/shard_map/ppermute | solution.py:304
  202.4 9.7 %collective-permute-start.17 = (bf16[2,2,2,24,768]{4,3,2,1,0:T(8,128)(2,1)S(1)}, bf16[2,2,2,24,768]{4,3,2,1,0:T(8,128)(2,1)S(1)}, u32[]{:S(2)}, u32[]{:S(2)}) collective-permute-start(bf16[2,2,2,24,768]{4,3,2,1,0:T(8,128)(2,1)S(1)} %copy.182), channel_id=1, source_target_pairs={{0,4},{2,6},{4,0},{6,2},{8,12},{10,14},{12,8},{14,10},{16,20},{18,... | collective-permute-start | bytes 884744 | tf_op jit(solution)/shard_map/ppermute | solution.py:304
  204.6 10.2 %collective-permute-start.23 = (bf16[2,2,2,24,768]{4,3,2,1,0:T(8,128)(2,1)S(1)}, bf16[2,2,2,24,768]{4,3,2,1,0:T(8,128)(2,1)S(1)}, u32[]{:S(2)}, u32[]{:S(2)}) collective-permute-start(bf16[2,2,2,24,768]{4,3,2,1,0:T(8,128)(2,1)S(1)} %copy.189), channel_id=1, source_target_pairs={{0,8},{2,10},{4,12},{6,14},{8,0},{10,2},{12,4},{14,6},{16,24},{18,... | collective-permute-start | bytes 884744 | tf_op jit(solution)/shard_map/ppermute | solution.py:304
  206.5 14.4 %collective-permute-start.29 = (bf16[2,2,2,24,768]{4,3,2,1,0:T(8,128)(2,1)S(1)}, bf16[2,2,2,24,768]{4,3,2,1,0:T(8,128)(2,1)S(1)}, u32[]{:S(2)}, u32[]{:S(2)}) collective-permute-start(bf16[2,2,2,24,768]{4,3,2,1,0:T(8,128)(2,1)S(1)} %copy.196), channel_id=1, source_target_pairs={{0,8},{2,10},{4,12},{6,14},{8,0},{10,2},{12,4},{14,6},{16,24},{18,... | collective-permute-start | bytes 884744 | tf_op jit(solution)/shard_map/ppermute | solution.py:304
  210.9 35.5 %collective-permute-start.40 = (bf16[2,2,2,2,96,768]{5,4,0,3,2,1:T(8,128)(2,1)S(1)}, bf16[2,2,2,2,96,768]{5,4,0,3,2,1:T(8,128)(2,1)S(1)}, u32[]{:S(2)}, u32[]{:S(2)}) collective-permute-start(bf16[2,2,2,2,96,768]{5,4,0,3,2,1:T(8,128)(2,1)S(1)} %copy-done.11), channel_id=1, source_target_pairs={{0,1},{1,0},{2,3},{3,2},{4,5},{5,4},{6,7},{7,6},{8,9},{9,8},{10,11... | collective-permute-start | bytes 7077896 | tf_op jit(solution)/shard_map/ppermute | solution.py:298
  212.1 12.0 %collective-permute-start.6 = (bf16[2,2,24,768]{3,2,1,0:T(8,128)(2,1)S(1)}, bf16[2,2,24,768]{3,2,1,0:T(8,128)(2,1)S(1)}, u32[]{:S(2)}, u32[]{:S(2)}) collective-permute-start(bf16[2,2,24,768]{3,2,1,0:T(8,128)(2,1)S(1)} %copy.175), channel_id=1, source_target_pairs={{0,4},{2,6},{4,0},{6,2},{8,12},{10,14},{12,8},{14,10},{16,20},{18,... | collective-permute-start | bytes 442376 | tf_op jit(solution)/shard_map/ppermute | solution.py:304
  214.9 10.5 %collective-permute-start.18 = (bf16[2,2,24,768]{3,2,1,0:T(8,128)(2,1)S(1)}, bf16[2,2,24,768]{3,2,1,0:T(8,128)(2,1)S(1)}, u32[]{:S(2)}, u32[]{:S(2)}) collective-permute-start(bf16[2,2,24,768]{3,2,1,0:T(8,128)(2,1)S(1)} %copy.185), channel_id=1, source_target_pairs={{0,8},{2,10},{4,12},{6,14},{8,0},{10,2},{12,4},{14,6},{16,24},{18,... | collective-permute-start | bytes 442376 | tf_op jit(solution)/shard_map/ppermute | solution.py:304
  222.0 6.4 %collective-permute-start.24 = (bf16[2,2,24,768]{3,2,1,0:T(8,128)(2,1)S(1)}, bf16[2,2,24,768]{3,2,1,0:T(8,128)(2,1)S(1)}, u32[]{:S(2)}, u32[]{:S(2)}) collective-permute-start(bf16[2,2,24,768]{3,2,1,0:T(8,128)(2,1)S(1)} %copy.192), channel_id=1, source_target_pairs={{0,2},{2,0},{4,6},{6,4},{8,10},{10,8},{12,14},{14,12},{16,18},{18,... | collective-permute-start | bytes 442376 | tf_op jit(solution)/shard_map/ppermute | solution.py:304
  224.2 6.8 %collective-permute-start.30 = (bf16[2,2,24,768]{3,2,1,0:T(8,128)(2,1)S(1)}, bf16[2,2,24,768]{3,2,1,0:T(8,128)(2,1)S(1)}, u32[]{:S(2)}, u32[]{:S(2)}) collective-permute-start(bf16[2,2,24,768]{3,2,1,0:T(8,128)(2,1)S(1)} %copy.199), channel_id=1, source_target_pairs={{0,2},{2,0},{4,6},{6,4},{8,10},{10,8},{12,14},{14,12},{16,18},{18,... | collective-permute-start | bytes 442376 | tf_op jit(solution)/shard_map/ppermute | solution.py:304
  225.4 6.3 %collective-permute-start.7 = (bf16[2,24,768]{2,1,0:T(8,128)(2,1)S(1)}, bf16[2,24,768]{2,1,0:T(8,128)(2,1)S(1)}, u32[]{:S(2)}, u32[]{:S(2)}) collective-permute-start(bf16[2,24,768]{2,1,0:T(8,128)(2,1)S(1)} %fusion.41), channel_id=1, source_target_pairs={{0,8},{2,10},{4,12},{6,14},{8,0},{10,2},{12,4},{14,6},{16,24},{18,... | collective-permute-start | bytes 221192 | tf_op jit(solution)/shard_map/ppermute | solution.py:304
  228.4 5.7 %collective-permute-start.19 = (bf16[2,24,768]{2,1,0:T(8,128)(2,1)S(1)}, bf16[2,24,768]{2,1,0:T(8,128)(2,1)S(1)}, u32[]{:S(2)}, u32[]{:S(2)}) collective-permute-start(bf16[2,24,768]{2,1,0:T(8,128)(2,1)S(1)} %fusion.40), channel_id=1, source_target_pairs={{0,2},{2,0},{4,6},{6,4},{8,10},{10,8},{12,14},{14,12},{16,18},{18,... | collective-permute-start | bytes 221192 | tf_op jit(solution)/shard_map/ppermute | solution.py:304
  231.0 5.0 %collective-permute-start.25 = (bf16[2,24,768]{2,1,0:T(8,128)(2,1)S(1)}, bf16[2,24,768]{2,1,0:T(8,128)(2,1)S(1)}, u32[]{:S(2)}, u32[]{:S(2)}) collective-permute-start(bf16[2,24,768]{2,1,0:T(8,128)(2,1)S(1)} %fusion.39), channel_id=1, source_target_pairs={{0,4},{2,6},{4,0},{6,2},{8,12},{10,14},{12,8},{14,10},{16,20},{18,... | collective-permute-start | bytes 221192 | tf_op jit(solution)/shard_map/ppermute | solution.py:304
  231.7 7.4 %collective-permute-start.31 = (bf16[2,24,768]{2,1,0:T(8,128)(2,1)S(1)}, bf16[2,24,768]{2,1,0:T(8,128)(2,1)S(1)}, u32[]{:S(2)}, u32[]{:S(2)}) collective-permute-start(bf16[2,24,768]{2,1,0:T(8,128)(2,1)S(1)} %fusion.38), channel_id=1, source_target_pairs={{0,4},{2,6},{4,0},{6,2},{8,12},{10,14},{12,8},{14,10},{16,20},{18,... | collective-permute-start | bytes 221192 | tf_op jit(solution)/shard_map/ppermute | solution.py:304
  234.2 5.8 %collective-permute-start.8 = (bf16[24,768]{1,0:T(8,128)(2,1)S(1)}, bf16[24,768]{1,0:T(8,128)(2,1)S(1)}, u32[]{:S(2)}, u32[]{:S(2)}) collective-permute-start(bf16[24,768]{1,0:T(8,128)(2,1)S(1)} %fusion.48), channel_id=1, source_target_pairs={{0,16},{2,18},{4,20},{6,22},{8,24},{10,26},{12,28},{14,30},{16,0},... | collective-permute-start | bytes 110600 | tf_op jit(solution)/shard_map/ppermute | solution.py:304
  236.0 7.6 %collective-permute-start.20 = (bf16[24,768]{1,0:T(8,128)(2,1)S(1)}, bf16[24,768]{1,0:T(8,128)(2,1)S(1)}, u32[]{:S(2)}, u32[]{:S(2)}) collective-permute-start(bf16[24,768]{1,0:T(8,128)(2,1)S(1)} %fusion.46), channel_id=1, source_target_pairs={{0,16},{2,18},{4,20},{6,22},{8,24},{10,26},{12,28},{14,30},{16,0},... | collective-permute-start | bytes 110600 | tf_op jit(solution)/shard_map/ppermute | solution.py:304
  239.1 6.1 %collective-permute-start.26 = (bf16[24,768]{1,0:T(8,128)(2,1)S(1)}, bf16[24,768]{1,0:T(8,128)(2,1)S(1)}, u32[]{:S(2)}, u32[]{:S(2)}) collective-permute-start(bf16[24,768]{1,0:T(8,128)(2,1)S(1)} %fusion.44), channel_id=1, source_target_pairs={{0,16},{2,18},{4,20},{6,22},{8,24},{10,26},{12,28},{14,30},{16,0},... | collective-permute-start | bytes 110600 | tf_op jit(solution)/shard_map/ppermute | solution.py:304
  240.0 7.1 %collective-permute-start.32 = (bf16[24,768]{1,0:T(8,128)(2,1)S(1)}, bf16[24,768]{1,0:T(8,128)(2,1)S(1)}, u32[]{:S(2)}, u32[]{:S(2)}) collective-permute-start(bf16[24,768]{1,0:T(8,128)(2,1)S(1)} %fusion.42), channel_id=1, source_target_pairs={{0,16},{2,18},{4,20},{6,22},{8,24},{10,26},{12,28},{14,30},{16,0},... | collective-permute-start | bytes 110600 | tf_op jit(solution)/shard_map/ppermute | solution.py:304
  243.1 5.0 %collective-permute-start.9 = (f32[24,768]{1,0:T(8,128)S(1)}, f32[24,768]{1,0:T(8,128)S(1)}, u32[]{:S(2)}, u32[]{:S(2)}) collective-permute-start(f32[24,768]{1,0:T(8,128)S(1)} %fusion.49), channel_id=1, source_target_pairs={{0,1},{1,0},{2,3},{3,2},{4,5},{5,4},{6,7},{7,6},{8,9},{9,8},{10,11... | collective-permute-start | bytes 221192 | tf_op jit(solution)/shard_map/ppermute | solution.py:308
  243.6 28.4 %collective-permute-start.35 = (bf16[2,2,2,24,3072]{4,3,2,1,0:T(8,128)(2,1)S(1)}, bf16[2,2,2,24,3072]{4,3,2,1,0:T(8,128)(2,1)S(1)}, u32[]{:S(2)}, u32[]{:S(2)}) collective-permute-start(bf16[2,2,2,24,3072]{4,3,2,1,0:T(8,128)(2,1)S(1)} %copy.203), channel_id=1, source_target_pairs={{0,4},{2,6},{4,0},{6,2},{8,12},{10,14},{12,8},{14,10},{16,20},{18,... | collective-permute-start | bytes 3538952 | tf_op jit(solution)/shard_map/ppermute | solution.py:304
  245.2 3.0 collective-permute-start.21
  246.4 27.1 %collective-permute-start.27 = (f32[24,768]{1,0:T(8,128)S(1)}, f32[24,768]{1,0:T(8,128)S(1)}, u32[]{:S(2)}, u32[]{:S(2)}) collective-permute-start(f32[24,768]{1,0:T(8,128)S(1)} %fusion.45), channel_id=1, source_target_pairs={{0,1},{1,0},{2,3},{3,2},{4,5},{5,4},{6,7},{7,6},{8,9},{9,8},{10,11... | collective-permute-start | bytes 221192 | tf_op jit(solution)/shard_map/ppermute | solution.py:308
  247.2 28.1 %collective-permute-start.41 = (bf16[2,2,2,96,768]{4,3,2,1,0:T(8,128)(2,1)S(1)}, bf16[2,2,2,96,768]{4,3,2,1,0:T(8,128)(2,1)S(1)}, u32[]{:S(2)}, u32[]{:S(2)}) collective-permute-start(bf16[2,2,2,96,768]{4,3,2,1,0:T(8,128)(2,1)S(1)} %copy.210), channel_id=1, source_target_pairs={{0,2},{2,0},{4,6},{6,4},{8,10},{10,8},{12,14},{14,12},{16,18},{18,... | collective-permute-start | bytes 3538952 | tf_op jit(solution)/shard_map/ppermute | solution.py:304
  248.1 39.8 %collective-permute-start.33 = (f32[24,768]{1,0:T(8,128)S(1)}, f32[24,768]{1,0:T(8,128)S(1)}, u32[]{:S(2)}, u32[]{:S(2)}) collective-permute-start(f32[24,768]{1,0:T(8,128)S(1)} %fusion.43), channel_id=1, source_target_pairs={{0,1},{1,0},{2,3},{3,2},{4,5},{5,4},{6,7},{7,6},{8,9},{9,8},{10,11... | collective-permute-start | bytes 221192 | tf_op jit(solution)/shard_map/ppermute | solution.py:308
  272.2 14.9 %collective-permute-start.36 = (bf16[2,2,24,3072]{3,2,1,0:T(8,128)(2,1)S(1)}, bf16[2,2,24,3072]{3,2,1,0:T(8,128)(2,1)S(1)}, u32[]{:S(2)}, u32[]{:S(2)}) collective-permute-start(bf16[2,2,24,3072]{3,2,1,0:T(8,128)(2,1)S(1)} %copy.206), channel_id=1, source_target_pairs={{0,8},{2,10},{4,12},{6,14},{8,0},{10,2},{12,4},{14,6},{16,24},{18,... | collective-permute-start | bytes 1769480 | tf_op jit(solution)/shard_map/ppermute | solution.py:304
  275.5 14.6 %collective-permute-start.42 = (bf16[2,2,96,768]{3,2,1,0:T(8,128)(2,1)S(1)}, bf16[2,2,96,768]{3,2,1,0:T(8,128)(2,1)S(1)}, u32[]{:S(2)}, u32[]{:S(2)}) collective-permute-start(bf16[2,2,96,768]{3,2,1,0:T(8,128)(2,1)S(1)} %copy.213), channel_id=1, source_target_pairs={{0,4},{2,6},{4,0},{6,2},{8,12},{10,14},{12,8},{14,10},{16,20},{18,... | collective-permute-start | bytes 1769480 | tf_op jit(solution)/shard_map/ppermute | solution.py:304
  287.3 7.7 %collective-permute-start.37 = (bf16[2,24,3072]{2,1,0:T(8,128)(2,1)S(1)}, bf16[2,24,3072]{2,1,0:T(8,128)(2,1)S(1)}, u32[]{:S(2)}, u32[]{:S(2)}) collective-permute-start(bf16[2,24,3072]{2,1,0:T(8,128)(2,1)S(1)} %fusion.25), channel_id=1, source_target_pairs={{0,2},{2,0},{4,6},{6,4},{8,10},{10,8},{12,14},{14,12},{16,18},{18,... | collective-permute-start | bytes 884744 | tf_op jit(solution)/shard_map/ppermute | solution.py:304
  290.3 8.6 %collective-permute-start.43 = (bf16[2,96,768]{2,1,0:T(8,128)(2,1)S(1)}, bf16[2,96,768]{2,1,0:T(8,128)(2,1)S(1)}, u32[]{:S(2)}, u32[]{:S(2)}) collective-permute-start(bf16[2,96,768]{2,1,0:T(8,128)(2,1)S(1)} %fusion.24), channel_id=1, source_target_pairs={{0,8},{2,10},{4,12},{6,14},{8,0},{10,2},{12,4},{14,6},{16,24},{18,... | collective-permute-start | bytes 884744 | tf_op jit(solution)/shard_map/ppermute | solution.py:304
  295.1 12.4 %collective-permute-start.38 = (bf16[24,3072]{1,0:T(8,128)(2,1)S(1)}, bf16[24,3072]{1,0:T(8,128)(2,1)S(1)}, u32[]{:S(2)}, u32[]{:S(2)}) collective-permute-start(bf16[24,3072]{1,0:T(8,128)(2,1)S(1)} %fusion.32), channel_id=1, source_target_pairs={{0,16},{2,18},{4,20},{6,22},{8,24},{10,26},{12,28},{14,30},{16,0},... | collective-permute-start | bytes 442376 | tf_op jit(solution)/shard_map/ppermute | solution.py:304
  299.0 10.2 %collective-permute-start.44 = (bf16[96,768]{1,0:T(8,128)(2,1)S(1)}, bf16[96,768]{1,0:T(8,128)(2,1)S(1)}, u32[]{:S(2)}, u32[]{:S(2)}) collective-permute-start(bf16[96,768]{1,0:T(8,128)(2,1)S(1)} %fusion.30), channel_id=1, source_target_pairs={{0,16},{2,18},{4,20},{6,22},{8,24},{10,26},{12,28},{14,30},{16,0},... | collective-permute-start | bytes 442376 | tf_op jit(solution)/shard_map/ppermute | solution.py:304
  307.6 1.7 collective-permute-start.39
  309.3 1.6 collective-permute-start.45
  (69 other events, 730.3 us)
